TPU v7x, 256 devices: a whole 4x4x8 slice. The times are simulated.
256 devices in a mesh: lat: 64 (over z, x, core), dep: 4 (over y).
Axes of the slice: x: 4, y: 4, z: 8, core: 2. Of those that a mesh axis runs over, the one named last changes fastest.
Arguments:
- kernel: bfloat16 [131072, 64, 128], P(('lat', 'dep')), may hold values from -0.1875 to 0.1875
- coefficient: float32 [131072, 256], P(('lat', 'dep')), may hold values from -3 to 3
- observed: float32 [16384, 64], P(('lat', 'dep')), may hold values from -6 to 6
- ray_brick: int32 [131072, 1], P(('lat', 'dep')), may hold values from 0 to 255; in each aligned block of 512 rows (0 to 511, 512 to 1023, ...) at most 3 rows name the same one
- tile_index: int32 [131072], P(('lat', 'dep')), may hold values from 0 to 511
- ray_count: int32 [256], P(('lat', 'dep')), may hold values from 32 to 64, as said below
- earth_model: float32 [256, 4, 512, 128], P(('lat', 'dep')), may hold values from -6 to 6
Outputs:
- residual: float32 [16384, 64], P(('lat', 'dep'))
- gradient: float32 [256, 4, 512, 128], P(('lat', 'dep'))
Inputs may be any that keep to these rules, and one draw needn't show every extreme that they name: `ray_brick`: among the hits of one device no brick is named more than 3 times, a bound that some block reaches. `ray_count`: the largest count is exactly 64.
All inputs are finite; a program needn't handle non-finite values.
Results may differ from a plain program's by a relative error of at most 0.0037.
Values may be sent and summed in bfloat16 or wider, within the bound.
No kernel may reach another device: no remote copies, remote signals or barrier semaphores. Data moves between devices by JAX's collectives and lax.ppermute only.
A program may use at most 64 MiB of HBM per device.

v0:
```python
import jax
import jax.numpy as jnp
from jax import lax
from jax.sharding import PartitionSpec as P


def per_device(kernel, coefficient, observed, ray_brick, tile_index, ray_count, earth_model):
    hit_count, band_count, cell_count = kernel.shape
    param_count = earth_model.shape[1]
    tile_count = earth_model.shape[2]
    ray_rows = observed.shape[0]
    per_ray = hit_count // ray_rows
    lat_count = lax.axis_size("lat")
    dep_count = lax.axis_size("dep")
    device_count = lat_count * dep_count
    slot_count = max(2, 3 * hit_count // (2 * device_count))
    slot_total = device_count * slot_count
    target = ray_brick[:, 0]
    live_rays = jnp.arange(ray_rows) < ray_count[0]
    live_hits = jnp.repeat(live_rays, per_ray)
    hit_order = jnp.arange(hit_count)
    earlier = (
        (target[None, :] == target[:, None])
        & (hit_order[None, :] < hit_order[:, None])
        & live_hits[None, :]
    )
    rank_within = jnp.sum(earlier.astype(jnp.int32), axis=1)
    slot_of_hit = jnp.where(live_hits, target * slot_count + rank_within, slot_total)
    wanted = jnp.zeros((slot_total,), jnp.int32).at[slot_of_hit].set(tile_index + 1, mode="drop")
    wanted = wanted.reshape(lat_count, dep_count, slot_count)
    model_low = earth_model[0].astype(jnp.bfloat16)
    requests = lax.all_to_all(
        lax.all_to_all(wanted, "lat", split_axis=0, concat_axis=0, tiled=True),
        "dep",
        split_axis=1,
        concat_axis=1,
        tiled=True,
    )
    lookup = jnp.maximum(requests - 1, 0)
    blocks = jnp.take(model_low, lookup.reshape(-1), axis=1)
    blocks = blocks.reshape(param_count, lat_count, dep_count, slot_count, cell_count)
    arrived = lax.all_to_all(
        lax.all_to_all(blocks, "lat", split_axis=1, concat_axis=1, tiled=True),
        "dep",
        split_axis=2,
        concat_axis=2,
        tiled=True,
    )
    own_blocks = jnp.take(
        arrived.reshape(param_count, slot_total, cell_count),
        jnp.minimum(slot_of_hit, slot_total - 1),
        axis=1,
    )
    coefficient_split = coefficient.reshape(hit_count, param_count, band_count)
    sensitivity = jnp.einsum("hbc,phc->hpb", kernel, own_blocks, preferred_element_type=jnp.float32)
    contribution = jnp.sum(coefficient_split * sensitivity, axis=1)
    predicted = jnp.sum(contribution.reshape(ray_rows, per_ray, band_count), axis=1)
    residual = jnp.where(live_rays[:, None], predicted - observed, jnp.zeros_like(predicted))
    residual_hit = jnp.repeat(residual, per_ray, axis=0)
    weight = (coefficient_split * residual_hit[:, None, :]).astype(jnp.bfloat16)
    gradient_term = jnp.einsum("hpb,hbc->phc", weight, kernel, preferred_element_type=jnp.float32)
    outgoing = (
        jnp.zeros((param_count, slot_total, cell_count), jnp.float32)
        .at[:, slot_of_hit]
        .set(gradient_term, mode="drop")
    )
    outgoing = outgoing.reshape(param_count, lat_count, dep_count, slot_count, cell_count)
    returned = lax.all_to_all(
        lax.all_to_all(outgoing, "lat", split_axis=1, concat_axis=1, tiled=True),
        "dep",
        split_axis=2,
        concat_axis=2,
        tiled=True,
    )
    segment = jnp.where(requests > 0, requests - 1, tile_count)
    brick_sum = jnp.zeros((param_count, tile_count + 1, cell_count), jnp.float32)
    brick_sum = brick_sum.at[:, segment.reshape(-1)].add(
        returned.reshape(param_count, slot_total, cell_count)
    )
    summed = brick_sum[:, :tile_count]
    return (residual, summed.reshape(1, param_count, tile_count, cell_count))


def solution(mesh):
    return jax.shard_map(
        per_device,
        mesh=mesh,
        in_specs=(
            P(("lat", "dep"), None, None),
            P(("lat", "dep"), None),
            P(("lat", "dep"), None),
            P(("lat", "dep"), None),
            P(("lat", "dep")),
            P(("lat", "dep")),
            P(("lat", "dep"), None, None, None),
        ),
        out_specs=(P(("lat", "dep"), None), P(("lat", "dep"), None, None, None)),
        check_vma=False,
    )
```

profile of v0, /device:TPU:1, one launch (start us, length us, event | category | flops | bytes accessed | tf_op | source)
XLA Modules:
  0.0 217.0 jit_solution(9075684628513270902)
XLA Ops:
  1.6 1.0 convert_reduce_fusion
  2.6 0.7 and_reduce_fusion
  3.3 0.7 broadcast_add_fusion
  4.0 2.4 %scatter_custom_fusion = s32[768]{0:T(1024)S(1)} fusion(s32[512]{0:T(512)S(1)} %bitcast.45, s32[512]{0:T(512)S(1)} %broadcast_add_fusion, s32[]{:T(128)} %constant.16.clone.1), kind=kCustom, calls=%fused_computation.34 | custom fusion | bytes 3076 | tf_op jit(solution)/shard_map/scatter | solution.py:29
  6.7 23.9 %all_to_all.30 = s32[64,4,3]{2,1,0:T(4,128)S(1)} all-to-all(s32[64,4,3]{2,1,0:T(4,128)S(1)} %reshape.119), channel_id=1, replica_groups=mesh['lat'=64,'dep'=4] {'lat'}, dimensions={0} | all-to-all | bytes 6144 | tf_op jit(solution)/shard_map/all_to_all | solution.py:33
  30.7 0.7 reshape.172
  31.4 4.2 %all-to-all-start.1 = ((s32[4,1,192]{2,1,0:T(1,128)}), s32[4,1,192]{2,1,0:T(1,128)S(1)}, u32[]{:S(2)}, u32[]{:S(2)}) async-start(s32[4,1,192]{2,1,0:T(1,128)} %reshape.172), calls=%async_computation.1 | async-start | bytes 8192 | tf_op jit(solution)/shard_map/all_to_all | solution.py:32
  35.5 1.3 convert_element_type.16
  36.8 0.4 copy.79
  37.3 2.4 %all-to-all-done.1 = s32[4,1,192]{2,1,0:T(1,128)S(1)} async-done(((s32[4,1,192]{2,1,0:T(1,128)}), s32[4,1,192]{2,1,0:T(1,128)S(1)}, u32[]{:S(2)}, u32[]{:S(2)}) %all-to-all-start.1) | async-done | bytes 3104 | tf_op jit(solution)/shard_map/all_to_all | solution.py:32
  39.7 0.5 broadcast.120
  40.2 0.7 reduce.6
  41.5 2.8 %gather_fusion = bf16[768,4,128]{2,1,0:T(4,128)(2,1)S(1)} fusion(bf16[4,512,128]{2,0,1:T(4,128)(2,1)S(1)} %bitcast.38, s32[1024]{0:T(1024)S(1)} %pad_clamp_fusion.1), kind=kCustom, calls=%fused_computation | custom fusion | bytes 1575936 | tf_op jit(solution)/shard_map/jit(_take)/gather | solution.py:40
  44.4 1.1 broadcast_select_fusion
  45.5 28.2 %all_to_all.31 = bf16[4,64,4,3,128]{4,0,3,2,1:T(4,128)(2,1)S(1)} all-to-all(bf16[4,64,4,3,128]{4,0,3,2,1:T(4,128)(2,1)S(1)} %broadcast_select_fusion), channel_id=1, replica_groups=mesh['lat'=64,'dep'=4] {'lat'}, dimensions={1} | all-to-all | bytes 1572864 | tf_op jit(solution)/shard_map/all_to_all | solution.py:43
  73.8 1.2 copy.68
  74.9 3.7 %all-to-all-start.3 = ((bf16[4,64,4,3,128]{4,0,3,1,2:T(4,128)(2,1)}), bf16[4,64,4,3,128]{4,0,3,1,2:T(4,128)(2,1)S(1)}, u32[]{:S(2)}, u32[]{:S(2)}) async-start(bf16[4,64,4,3,128]{4,0,3,1,2:T(4,128)(2,1)} %copy.68), calls=%async_computation.3 | async-start | bytes 1572864 | tf_op jit(solution)/shard_map/all_to_all | solution.py:42
  78.8 0.4 copy.70
  79.2 10.8 %all-to-all-done.3 = bf16[4,64,4,3,128]{4,0,3,1,2:T(4,128)(2,1)S(1)} async-done(((bf16[4,64,4,3,128]{4,0,3,1,2:T(4,128)(2,1)}), bf16[4,64,4,3,128]{4,0,3,1,2:T(4,128)(2,1)S(1)}, u32[]{:S(2)}, u32[]{:S(2)}) %all-to-all-start.3) | async-done | bytes 786464 | tf_op jit(solution)/shard_map/all_to_all | solution.py:42
  90.1 0.3 copy.69
  90.3 2.1 gather_fusion.1
  92.4 7.0 %fusion = f32[512,64]{1,0:T(8,128)S(1)} fusion(f32[512,4,64]{2,1,0:T(4,128)S(1)} %copy.70, bf16[512,64,128]{2,1,0:T(8,128)(2,1)} %param.7, bf16[512,4,128]{2,1,0:T(4,128)(2,1)S(1)} %gather_fusion.1, pred[512]{0:T(512)(128)(4,1)S(1)} %get-tuple-element.16), kind=kOutput, calls=%fused_computation.6 | convolution fusion | flops 34045952 | bytes 9568768 | tf_op jit(solution)/shard_map/hbc,phc->hpb/dot_general | solution.py:55
  99.8 0.3 copy.73
  100.1 5.6 %fusion.12 = f32[512,4,128]{2,1,0:T(4,128)S(1)} fusion(bf16[512,4,64]{2,1,0:T(4,128)(2,1)S(1)} %copy.73, bf16[512,64,128]{2,1,0:T(8,128)(2,1)} %param.7), kind=kOutput, calls=%fused_computation.40 | convolution fusion | flops 33554432 | bytes 9699328 | tf_op jit(solution)/shard_map/hpb,hbc->phc/dot_general | solution.py:61
  106.0 14.0 %scatter_fusion = f32[4,768,128]{2,0,1:T(4,128)S(1)} fusion(f32[4,768,128]{2,0,1:T(4,128)S(1)} %broadcast_in_dim.67, s32[512]{0:T(512)S(1)} %bitcast.46, f32[512,4,128]{2,1,0:T(4,128)S(1)} %fusion.12), kind=kCustom, calls=%fused_computation.3 | custom fusion | bytes 3147776 | tf_op jit(solution)/shard_map/scatter | solution.py:65
  120.0 45.6 %all_to_all.32 = f32[4,64,4,3,128]{4,0,3,2,1:T(4,128)S(1)} all-to-all(f32[4,64,4,3,128]{4,0,3,2,1:T(4,128)S(1)} %bitcast.34), channel_id=1, replica_groups=mesh['lat'=64,'dep'=4] {'lat'}, dimensions={1} | all-to-all | bytes 3145728 | tf_op jit(solution)/shard_map/all_to_all | solution.py:69
  165.6 1.4 copy.74
  167.0 3.6 %all-to-all-start.5 = ((f32[4,64,4,3,128]{4,0,3,1,2:T(4,128)}), f32[4,64,4,3,128]{4,0,3,1,2:T(4,128)S(1)}, u32[]{:S(2)}, u32[]{:S(2)}) async-start(f32[4,64,4,3,128]{4,0,3,1,2:T(4,128)} %copy.74), calls=%async_computation.5 | async-start | bytes 3145728 | tf_op jit(solution)/shard_map/all_to_all | solution.py:68
  171.0 18.9 %all-to-all-done.5 = f32[4,64,4,3,128]{4,0,3,1,2:T(4,128)S(1)} async-done(((f32[4,64,4,3,128]{4,0,3,1,2:T(4,128)}), f32[4,64,4,3,128]{4,0,3,1,2:T(4,128)S(1)}, u32[]{:S(2)}, u32[]{:S(2)}) %all-to-all-start.5) | async-done | bytes 1572896 | tf_op jit(solution)/shard_map/all_to_all | solution.py:68
  189.9 0.3 copy.75
  190.3 25.6 %scatter_fusion.1 = f32[4,513,128]{2,0,1:T(4,128)S(1)} fusion(f32[4,513,128]{2,0,1:T(4,128)S(1)} %broadcast_in_dim.65, s32[768]{0:T(1024)S(1)} %fusion.8, f32[768,4,128]{2,1,0:T(4,128)S(1)} %bitcast.35), kind=kCustom, calls=%fused_computation.4 | custom fusion | flops 393216 | bytes 4721664 | tf_op jit(solution)/shard_map/scatter-add | solution.py:77
  216.0 1.0 copy.76
  (34 shorter events, 2.6 us)
Async XLA Ops:
  31.4 8.3 %all-to-all-start.1 = ((s32[4,1,192]{2,1,0:T(1,128)}), s32[4,1,192]{2,1,0:T(1,128)S(1)}, u32[]{:S(2)}, u32[]{:S(2)}) async-start(s32[4,1,192]{2,1,0:T(1,128)} %reshape.172), calls=%async_computation.1 | async-start | bytes 8192 | tf_op jit(solution)/shard_map/all_to_all | solution.py:32
  73.8 4.8 %copy-start = (f32[512,256]{1,0:T(8,128)S(1)}, f32[512,256]{1,0:T(8,128)}, u32[]{:S(2)}) copy-start(f32[512,256]{1,0:T(8,128)} %param.8) | copy-start | bytes 1572868
  74.9 15.2 %all-to-all-start.3 = ((bf16[4,64,4,3,128]{4,0,3,1,2:T(4,128)(2,1)}), bf16[4,64,4,3,128]{4,0,3,1,2:T(4,128)(2,1)S(1)}, u32[]{:S(2)}, u32[]{:S(2)}) async-start(bf16[4,64,4,3,128]{4,0,3,1,2:T(4,128)(2,1)} %copy.68), calls=%async_computation.3 | async-start | bytes 1572864 | tf_op jit(solution)/shard_map/all_to_all | solution.py:42
  92.4 7.1 %copy-start.2 = (f32[64,64]{1,0:T(8,128)S(1)}, f32[64,64]{1,0:T(8,128)}, u32[]{:S(2)}) copy-start(f32[64,64]{1,0:T(8,128)} %param.9) | copy-start | bytes 49156
  99.6 6.2 %copy-start.1 = (f32[64,64]{1,0:T(8,128)}, f32[64,64]{1,0:T(8,128)S(1)}, u32[]{:S(2)}) copy-start(f32[64,64]{1,0:T(8,128)S(1)} %subtract_select_fusion) | copy-start | bytes 49156
  167.0 22.8 %all-to-all-start.5 = ((f32[4,64,4,3,128]{4,0,3,1,2:T(4,128)}), f32[4,64,4,3,128]{4,0,3,1,2:T(4,128)S(1)}, u32[]{:S(2)}, u32[]{:S(2)}) async-start(f32[4,64,4,3,128]{4,0,3,1,2:T(4,128)} %copy.74), calls=%async_computation.5 | async-start | bytes 3145728 | tf_op jit(solution)/shard_map/all_to_all | solution.py:68
where the time goes:
time: 219 us; the launch traced here: 217 us
  blocking collectives  97.7 us (45%)
  waiting for transfers between devices  32.2 us (15%)
  other arithmetic  31.4 us (14%)
  local copies, waits for them, and re-layouts  30.2 us (14%)
  matrix products  12.6 us (6%)
  starting transfers between devices  11.4 us (5%)
    all_to_all x1, blocking collectives, per_device(): lax.all_to_all(outgoing, 'lat', split_axis=1, concat_axis=1, tiled=True)  45.6 us
    all_to_all x1, blocking collectives, per_device(): lax.all_to_all(blocks, 'lat', split_axis=1, concat_axis=1, tiled=True)  28.2 us
    scatter-add x1, other arithmetic, per_device(): brick_sum.at[:, segment.reshape(-1)]  25.6 us
    all_to_all x1, blocking collectives, per_device(): lax.all_to_all(wanted, 'lat', split_axis=0, concat_axis=0, tiled=True)  23.9 us
    all_to_all x1, waiting for transfers between devices, per_device(): lax.all_to_all(lax.all_to_all(outgoing, 'lat', split_axis=1, concat_axis=...  18.9 us
    scatter x1, local copies, waits for them, and re-layouts, per_device(): outgoing = jnp.zeros((param_count, slot_total, cell_count), jnp.float32)....  14 us
    all_to_all x1, waiting for transfers between devices, per_device(): lax.all_to_all(lax.all_to_all(blocks, 'lat', split_axis=1, concat_axis=1,...  10.8 us
    dot_general x1, matrix products, per_device(): jnp.einsum('hbc,phc->hpb', kernel, own_blocks, preferred_element_type=jnp...  6.97 us
  transfers between devices with their start and end apart: 3, of which 3 were waited for; matrix products, arithmetic and copies ran while one was open for 1% of the time, Pallas kernels for 0%

commit v1 on v0

v1 whole, which is shorter than its diff:
```python
import functools

import jax
import jax.numpy as jnp
from jax import lax
from jax.experimental import pallas as pl
from jax.experimental.pallas import tpu as pltpu
from jax.sharding import PartitionSpec as P

SLOTS = 3
AXES = ("lat", "dep")
VMEM = pl.BlockSpec(memory_space=pltpu.VMEM)
SMEM = pl.BlockSpec(memory_space=pltpu.SMEM)
ANY = pl.BlockSpec(memory_space=pl.ANY)


def iota(shape, axis):
    return lax.broadcasted_iota(jnp.int32, shape, axis)


def column_of(row):
    wide = jnp.broadcast_to(row.astype(jnp.float32), (128, row.shape[1]))
    return wide.T


def plan_kernel(count_ref, brick_ref, tile_ref, wanted_ref, slot_ref, *, per_ray, devices):
    hits = brick_ref.shape[1]
    live = count_ref[0] * per_ray
    brick = brick_ref[...].astype(jnp.float32)
    down = column_of(brick)
    ranks = []
    for start in range(0, hits, 128):
        across = brick[:, start : start + 128]
        first = iota((hits, 128), 0)
        earlier = (down == across) & (first < iota((hits, 128), 1) + start) & (first < live)
        ranks.append(jnp.sum(earlier.astype(jnp.float32), axis=0, keepdims=True))
    rank = jnp.concatenate(ranks, axis=1)
    alive = iota((1, hits), 1) < live
    slot = jnp.where(alive, rank * devices + brick, -1.0)
    slot_ref[...] = slot
    tile = tile_ref[...].astype(jnp.float32) + 1.0
    owner = iota((devices, 1), 0).astype(jnp.float32)
    lane = iota((devices, 128), 1)
    wanted = jnp.zeros((devices, 128), jnp.float32)
    for k in range(SLOTS):
        hit = jnp.where(slot == owner + float(k * devices), tile, 0.0)
        wanted = jnp.where(lane == k, jnp.sum(hit, axis=1, keepdims=True), wanted)
    wanted_ref[...] = wanted.astype(jnp.int32)


def spread(product, spread_ref, k, rows, params, cells):
    for p in range(params):
        spread_ref[pl.ds(k * params + p, rows, stride=SLOTS * params), :] = product[:, p * cells : (p + 1) * cells]


def gathered(spread_ref, k, rows, params):
    parts = [spread_ref[pl.ds(k * params + p, rows, stride=SLOTS * params), :] for p in range(params)]
    return jnp.concatenate(parts, axis=1).astype(jnp.bfloat16)


def fetch_kernel(wanted_ref, model_ref, out_ref, spread_ref):
    params, tiles, cells = model_ref.shape
    devices = wanted_ref.shape[0]
    model = jnp.concatenate([model_ref[p].astype(jnp.bfloat16) for p in range(params)], axis=1)
    wanted = wanted_ref[...]
    for k in range(SLOTS):
        pick = wanted[:, k : k + 1] == iota((devices, tiles), 1) + 1
        pick = pick.astype(jnp.float32).astype(jnp.bfloat16)
        product = jnp.dot(pick, model, preferred_element_type=jnp.float32)
        spread(product, spread_ref, k, devices, params, cells)
    out_ref[...] = spread_ref[...].astype(jnp.bfloat16)


def rays_kernel(
    count_ref, slot_ref, arrived_ref, coefficient_ref, observed_ref, kernel_ref,
    residual_ref, out_ref, spread_ref, own_ref, grad_ref, held_ref, sems, *, per_ray, params, chunks, group,
):
    hits, bands, cells = held_ref.shape
    rays = observed_ref.shape[0]
    devices = arrived_ref.shape[0] // (SLOTS * params)
    step = hits // chunks
    copies = [
        pltpu.make_async_copy(kernel_ref.at[pl.ds(i * step, step)], held_ref.at[pl.ds(i * step, step)], sems.at[i])
        for i in range(chunks)
    ]
    for copy in copies:
        copy.start()
    spread_ref[...] = arrived_ref[...].astype(jnp.float32)
    slot = slot_ref[...]
    slot_down = column_of(slot)
    picks = []
    for start in range(0, SLOTS * devices, 128):
        pick = slot_down == (iota((hits, 128), 1) + start).astype(jnp.float32)
        picks.append(pick.astype(jnp.float32).astype(jnp.bfloat16))
    pick = jnp.concatenate(picks, axis=1)
    blocks = jnp.concatenate([gathered(spread_ref, k, devices, params) for k in range(SLOTS)], axis=0)
    own_ref[...] = jnp.dot(pick, blocks, preferred_element_type=jnp.float32)

    lane = iota((per_ray, 128), 1)
    low = lane < bands
    pairs = per_ray * bands // 128
    mine = [iota((per_ray, 128), 0) == 2 * j + lane // bands for j in range(pairs)]
    live = count_ref[0]

    def one(ray):
        rows = pl.ds(pl.multiple_of(ray * per_ray, per_ray), per_ray)
        block = jnp.concatenate([own_ref[rows, p * cells : (p + 1) * cells] for p in range(params)], axis=0)
        sheet = held_ref[rows].reshape(per_ray * bands, cells)
        sense = lax.dot_general(
            block.astype(jnp.bfloat16), sheet, (((1,), (1,)), ((), ())), preferred_element_type=jnp.float32
        )
        scale = []
        for half in range(params // 2):
            two = coefficient_ref[rows, half * 128 : half * 128 + 128]
            turned = pltpu.roll(two, bands, 1)
            scale.append(jnp.where(low, two, turned))
            scale.append(jnp.where(low, turned, two))
        total = jnp.zeros((per_ray, 128), jnp.float32)
        for j in range(pairs):
            part = jnp.zeros((per_ray, 128), jnp.float32)
            for p in range(params):
                part += scale[p] * sense[p * per_ray : (p + 1) * per_ray, j * 128 : (j + 1) * 128]
            total += jnp.where(mine[j], part, 0.0)
        predicted = jnp.sum(total, axis=0, keepdims=True)
        predicted = predicted + pltpu.roll(predicted, bands, 1)
        seen = observed_ref[pl.ds(ray, 1), :]
        residual = jnp.where(ray < live, predicted - jnp.concatenate([seen, seen], axis=1), 0.0)
        residual_ref[pl.ds(ray, 1), :] = residual[:, :bands]
        weights = [p * residual for p in scale]
        weight = jnp.concatenate(
            [jnp.concatenate([jnp.where(mine[j], w, 0.0) for j in range(pairs)], axis=1) for w in weights], axis=0
        ).astype(jnp.bfloat16)
        term = jnp.dot(weight, sheet, preferred_element_type=jnp.float32)
        for p in range(params):
            grad_ref[rows, p * cells : (p + 1) * cells] = term[p * per_ray : (p + 1) * per_ray]

    rays_step = step // per_ray
    for i in range(chunks):
        copies[i].wait()

        def several(g, carry, i=i):
            for n in range(group):
                one(i * rays_step + g * group + n)
            return carry

        lax.fori_loop(0, rays_step // group, several, 0)

    grad = grad_ref[...].astype(jnp.bfloat16)
    for k in range(SLOTS):
        place = slot == (iota((devices, hits), 0) + k * devices).astype(jnp.float32)
        place = place.astype(jnp.float32).astype(jnp.bfloat16)
        product = jnp.dot(place, grad, preferred_element_type=jnp.float32)
        spread(product, spread_ref, k, devices, params, cells)
    out_ref[...] = spread_ref[...].astype(jnp.bfloat16)


def sum_kernel(wanted_ref, returned_ref, out_ref, spread_ref):
    params, tiles, cells = out_ref.shape
    devices = wanted_ref.shape[0]
    spread_ref[...] = returned_ref[...].astype(jnp.float32)
    across = wanted_ref[...].astype(jnp.float32).T
    picks = []
    for k in range(SLOTS):
        pick = across[k : k + 1, :] == (iota((tiles, devices), 0) + 1).astype(jnp.float32)
        picks.append(pick.astype(jnp.float32).astype(jnp.bfloat16))
    pick = jnp.concatenate(picks, axis=1)
    blocks = jnp.concatenate([gathered(spread_ref, k, devices, params) for k in range(SLOTS)], axis=0)
    for p in range(params):
        out_ref[p] = jnp.dot(pick, blocks[:, p * cells : (p + 1) * cells], preferred_element_type=jnp.float32)


def exchange(rows, devices, params, cells):
    sent = rows.reshape(devices, SLOTS, params, cells)
    back = lax.all_to_all(sent, AXES, split_axis=0, concat_axis=0, tiled=True)
    return back.reshape(devices * SLOTS * params, cells)


def per_device(kernel, coefficient, observed, ray_brick, tile_index, ray_count, earth_model):
    hits, bands, cells = kernel.shape
    params, tiles = earth_model.shape[1:3]
    rays = observed.shape[0]
    per_ray = hits // rays
    devices = lax.axis_size("lat") * lax.axis_size("dep")
    messages = devices * SLOTS * params
    f32, bf16 = jnp.float32, jnp.bfloat16
    shape = jax.ShapeDtypeStruct

    wanted, slot = pl.pallas_call(
        functools.partial(plan_kernel, per_ray=per_ray, devices=devices),
        out_shape=(shape((devices, 128), jnp.int32), shape((1, hits), f32)),
        in_specs=[SMEM, VMEM, VMEM],
        out_specs=(VMEM, VMEM),
        name="plan",
    )(ray_count, ray_brick.reshape(1, hits), tile_index.reshape(1, hits))
    requests = lax.all_to_all(wanted.reshape(devices, 1, 128), AXES, split_axis=0, concat_axis=0, tiled=True)
    requests = requests.reshape(devices, 128)
    blocks = pl.pallas_call(
        fetch_kernel,
        out_shape=shape((messages, cells), bf16),
        in_specs=[VMEM, VMEM],
        out_specs=VMEM,
        scratch_shapes=[pltpu.VMEM((messages, cells), f32)],
        name="fetch",
    )(requests, earth_model[0])
    arrived = exchange(blocks, devices, params, cells)
    chunks = 8
    residual, outgoing = pl.pallas_call(
        functools.partial(rays_kernel, per_ray=per_ray, params=params, chunks=chunks, group=8),
        out_shape=(shape((rays, bands), f32), shape((messages, cells), bf16)),
        in_specs=[SMEM, VMEM, VMEM, VMEM, VMEM, ANY],
        out_specs=(VMEM, VMEM),
        scratch_shapes=[
            pltpu.VMEM((messages, cells), f32),
            pltpu.VMEM((hits, params * cells), f32),
            pltpu.VMEM((hits, params * cells), f32),
            pltpu.VMEM((hits, bands, cells), bf16),
            pltpu.SemaphoreType.DMA((chunks,)),
        ],
        name="rays",
    )(ray_count, slot, arrived, coefficient, observed, kernel)
    returned = exchange(outgoing, devices, params, cells)
    gradient = pl.pallas_call(
        sum_kernel,
        out_shape=shape((params, tiles, cells), f32),
        in_specs=[VMEM, VMEM],
        out_specs=VMEM,
        scratch_shapes=[pltpu.VMEM((messages, cells), f32)],
        name="add",
    )(requests, returned)
    return residual, gradient[None]


def solution(mesh):
    return jax.shard_map(
        per_device,
        mesh=mesh,
        in_specs=(
            P(AXES, None, None),
            P(AXES, None),
            P(AXES, None),
            P(AXES, None),
            P(AXES),
            P(AXES),
            P(AXES, None, None, None),
        ),
        out_specs=(P(AXES, None), P(AXES, None, None, None)),
        check_vma=False,
    )
```

time: 219 us -> 123 us (0.56)
  waiting for transfers between devices: 32.2 us -> 0 us
  other arithmetic: 31.4 us -> 0 us
  local copies, waits for them, and re-layouts: 30.2 us -> 0 us
  Pallas kernels: 0 us -> 28.5 us
  matrix products: 12.6 us -> 0 us
  starting transfers between devices: 11.4 us -> 0 us
  blocking collectives: 97.7 us -> 92.8 us
    all_to_all x3 -> x0, waiting for transfers between devices: 32.2 us -> none  [the longest x1 18.9 us: per_device(): lax.all_to_all(lax.all_to_all(outgoing, 'lat', split_axis=1, concat_axis=...]
    pallas_call x0 -> x4, Pallas kernels: none -> 28.5 us  [the longest x1 20.6 us: per_device(): pl.pallas_call(functools.partial(rays_kernel, per_ray=per_ray, params=par...]
    scatter-add x1 -> x0, other arithmetic: 25.6 us -> none  [per_device(): brick_sum.at[:, segment.reshape(-1)]]
    scatter x2 -> x0, local copies, waits for them, and re-layouts: 16.5 us -> none  [the longest x1 14 us: per_device(): outgoing = jnp.zeros((param_count, slot_total, cell_count), jnp.float32)....]
    dot_general x2 -> x0, matrix products: 12.6 us -> none  [the longest x1 6.97 us: per_device(): jnp.einsum('hbc,phc->hpb', kernel, own_blocks, preferred_element_type=jnp...]
    all_to_all x3 -> x0, starting transfers between devices: 11.4 us -> none  [the longest x1 4.18 us: per_device(): lax.all_to_all(lax.all_to_all(wanted, 'lat', split_axis=0, concat_axis=0,...]
    gather x2 -> x0, local copies, waits for them, and re-layouts: 4.93 us -> none  [the longest x1 2.84 us: per_device(): blocks = jnp.take(model_low, lookup.reshape(-1), axis=1)]
    all_to_all x3, blocking collectives: 97.7 us -> 92.8 us  [the longest x2 64.1 us: exchange(): back = lax.all_to_all(sent, AXES, split_axis=0, concat_axis=0, tiled=True)]
  transfers between devices with their start and end apart: 3 -> 0, of which waited for: 3 -> 0; matrix products, arithmetic and copies ran while one was open for 1% -> 0% of each run, Pallas kernels for 0% -> 0%
where the time goes in v1:
time: 123 us
  blocking collectives  92.8 us (75%)
  Pallas kernels  28.5 us (23%)
  between operations  1.29 us (1%)
    all_to_all x2, blocking collectives, exchange(): back = lax.all_to_all(sent, AXES, split_axis=0, concat_axis=0, tiled=True)  64.1 us
    all_to_all x1, blocking collectives, per_device(): lax.all_to_all(wanted.reshape(devices, 1, 128), AXES, split_axis=0, conca...  28.7 us
    pallas_call x1, Pallas kernels, per_device(): pl.pallas_call(functools.partial(rays_kernel, per_ray=per_ray, params=par...  20.6 us
    pallas_call x1, Pallas kernels, per_device(): pl.pallas_call(sum_kernel, out_shape=shape((params, tiles, cells), f32),...  3.27 us
    pallas_call x1, Pallas kernels, per_device(): pl.pallas_call(fetch_kernel, out_shape=shape((messages, cells), bf16), in...  2.86 us

profile of v1, /device:TPU:1, one launch (start us, length us, event | category | flops | bytes accessed | tf_op | source)
XLA Modules:
  0.0 122.6 jit_solution(16220221948247638419)
XLA Ops:
  1.3 1.7 %plan.1 = (s32[256,128]{1,0:T(8,128)}, f32[1,512]{1,0:T(1,128)}) custom-call(s32[1]{0:T(128)S(6)} %copy.10.count_ref, s32[1,512]{1,0:T(1,128)} %bitcast.21, s32[1,512]{1,0:T(1,128)} %bitcast.22), custom_call_target="tpu_custom_call" | custom-call | tf_op jit(solution)/shard_map/plan/pallas_call | solution.py:188
  3.0 28.7 %all_to_all.15 = s32[256,1,128]{2,1,0:T(1,128)} all-to-all(s32[256,1,128]{2,1,0:T(1,128)} %bitcast.20), channel_id=1, replica_groups=mesh['lat'=64,'dep'=4] {'lat','dep'}, dimensions={0} | all-to-all | bytes 262144 | tf_op jit(solution)/shard_map/all_to_all | solution.py:195
  31.7 2.9 %fetch.1 = bf16[3072,128]{1,0:T(8,128)(2,1)} custom-call(s32[256,128]{1,0:T(8,128)} %bitcast.15, f32[4,512,128]{2,1,0:T(8,128)} %bitcast.17), custom_call_target="tpu_custom_call" | custom-call | tf_op jit(solution)/shard_map/fetch/pallas_call | solution.py:197
  34.6 32.1 %all_to_all.16 = bf16[256,3,4,128]{3,2,1,0:T(4,128)(2,1)} all-to-all(bf16[256,3,4,128]{3,2,1,0:T(4,128)(2,1)} %bitcast.13), channel_id=1, replica_groups=mesh['lat'=64,'dep'=4] {'lat','dep'}, dimensions={0} | all-to-all | bytes 1572864 | tf_op jit(solution)/shard_map/all_to_all | solution.py:174
  66.7 20.6 %rays.1 = (f32[64,64]{1,0:T(8,128)}, bf16[3072,128]{1,0:T(8,128)(2,1)}) custom-call(s32[1]{0:T(128)S(6)} %copy.10.count_ref, f32[1,512]{1,0:T(1,128)} %get-tuple-element.6.slot_ref, bf16[3072,128]{1,0:T(8,128)(2,1)} %bitcast.14, f32[512,256]{1,0:T(8,128)} %coefficient_ref.1, f32[64,64]{1,0:T(8,128)} %observed_ref.1, bf16[512,64,128]{2,1,0:T(8,128)(2,1)} %kernel_ref.1), custom_call_target="tpu_custom_call" | custom-call | tf_op jit(solution)/shard_map/rays/pallas_call | solution.py:207
  87.3 32.0 %all_to_all.17 = bf16[256,3,4,128]{3,2,1,0:T(4,128)(2,1)} all-to-all(bf16[256,3,4,128]{3,2,1,0:T(4,128)(2,1)} %bitcast.19), channel_id=1, replica_groups=mesh['lat'=64,'dep'=4] {'lat','dep'}, dimensions={0} | all-to-all | bytes 1572864 | tf_op jit(solution)/shard_map/all_to_all | solution.py:174
  119.3 3.3 %add.1 = f32[4,512,128]{2,1,0:T(8,128)} custom-call(s32[256,128]{1,0:T(8,128)} %bitcast.16, bf16[3072,128]{1,0:T(8,128)(2,1)} %bitcast.12), custom_call_target="tpu_custom_call" | custom-call | tf_op jit(solution)/shard_map/add/pallas_call | solution.py:222

commit v2 on v1

v2 whole, which is shorter than its diff:
```python
import functools

import jax
import jax.numpy as jnp
from jax import lax
from jax.experimental import pallas as pl
from jax.experimental.pallas import tpu as pltpu
from jax.sharding import PartitionSpec as P

SLOTS = 3
MIB = 1 << 20
AXES = ("lat", "dep")
VMEM = pl.BlockSpec(memory_space=pltpu.VMEM)
SMEM = pl.BlockSpec(memory_space=pltpu.SMEM)
HBM = pl.BlockSpec(memory_space=pltpu.HBM)


def in_hbm(array):
    return pltpu.with_memory_space_constraint(array, pltpu.HBM)


def iota(shape, axis):
    return lax.broadcasted_iota(jnp.int32, shape, axis)


def column_of(row):
    wide = jnp.broadcast_to(row.astype(jnp.float32), (128, row.shape[1]))
    return wide.T


def plan_kernel(
    count_ref, brick_hbm, tile_hbm, wanted_ref, slot_ref, brick_ref, tile_ref, sems, *, per_ray, devices
):
    brick_copy = pltpu.make_async_copy(brick_hbm, brick_ref, sems.at[0])
    tile_copy = pltpu.make_async_copy(tile_hbm, tile_ref, sems.at[1])
    brick_copy.start()
    tile_copy.start()
    hits = brick_ref.shape[1]
    live = count_ref[0] * per_ray
    brick_copy.wait()
    tile_copy.wait()
    brick = brick_ref[...].astype(jnp.float32)
    down = column_of(brick)
    ranks = []
    for start in range(0, hits, 128):
        across = brick[:, start : start + 128]
        first = iota((hits, 128), 0)
        earlier = (down == across) & (first < iota((hits, 128), 1) + start) & (first < live)
        ranks.append(jnp.sum(earlier.astype(jnp.float32), axis=0, keepdims=True))
    rank = jnp.concatenate(ranks, axis=1)
    alive = iota((1, hits), 1) < live
    slot = jnp.where(alive, rank * devices + brick, -1.0)
    slot_ref[...] = slot
    tile = tile_ref[...].astype(jnp.float32) + 1.0
    owner = iota((devices, 1), 0).astype(jnp.float32)
    lane = iota((devices, 128), 1)
    wanted = jnp.zeros((devices, 128), jnp.float32)
    for k in range(SLOTS):
        hit = jnp.where(slot == owner + float(k * devices), tile, 0.0)
        wanted = jnp.where(lane == k, jnp.sum(hit, axis=1, keepdims=True), wanted)
    wanted_ref[...] = wanted.astype(jnp.int32)


def spread(product, spread_ref, k, rows, params, cells):
    for p in range(params):
        spread_ref[pl.ds(k * params + p, rows, stride=SLOTS * params), :] = product[:, p * cells : (p + 1) * cells]


def gathered(spread_ref, k, rows, params):
    parts = [spread_ref[pl.ds(k * params + p, rows, stride=SLOTS * params), :] for p in range(params)]
    return jnp.concatenate(parts, axis=1).astype(jnp.bfloat16)


def round_kernel(model_ref, low_ref):
    params, _, cells = model_ref.shape
    for p in range(params):
        low_ref[:, p * cells : (p + 1) * cells] = model_ref[p].astype(jnp.bfloat16)


def fetch_kernel(wanted_ref, model_ref, out_ref, spread_ref, *, params):
    tiles = model_ref.shape[0]
    cells = model_ref.shape[1] // params
    devices = wanted_ref.shape[0]
    model = model_ref[...]
    wanted = wanted_ref[...]
    for k in range(SLOTS):
        pick = wanted[:, k : k + 1] == iota((devices, tiles), 1) + 1
        pick = pick.astype(jnp.float32).astype(jnp.bfloat16)
        product = jnp.dot(pick, model, preferred_element_type=jnp.float32)
        spread(product, spread_ref, k, devices, params, cells)
    out_ref[...] = spread_ref[...].astype(jnp.bfloat16)


def rays_kernel(
    count_ref, slot_ref, arrived_ref, coefficient_hbm, observed_hbm, kernel_ref,
    residual_ref, out_ref, coefficient_ref, observed_ref, spread_ref, own_ref, grad_ref, total_ref, twice_ref,
    held_ref, sems, small_sems,
    *, per_ray, params, group,
):
    hits, bands, cells = held_ref.shape
    rays = observed_ref.shape[0]
    devices = arrived_ref.shape[0] // (SLOTS * params)
    chunks = rays // group
    step = group * per_ray

    def fetch(i):
        part = pl.ds(i * step, step)
        return pltpu.make_async_copy(kernel_ref.at[part], held_ref.at[part], sems.at[i])

    coefficient_copy = pltpu.make_async_copy(coefficient_hbm, coefficient_ref, small_sems.at[0])
    observed_copy = pltpu.make_async_copy(observed_hbm, observed_ref, small_sems.at[1])
    coefficient_copy.start()
    for i in range(chunks):
        fetch(i).start()
    observed_copy.start()
    spread_ref[...] = arrived_ref[...].astype(jnp.float32)
    slot = slot_ref[...]
    slot_down = column_of(slot)
    picks = []
    for start in range(0, SLOTS * devices, 128):
        pick = slot_down == (iota((hits, 128), 1) + start).astype(jnp.float32)
        picks.append(pick.astype(jnp.float32).astype(jnp.bfloat16))
    pick = jnp.concatenate(picks, axis=1)
    blocks = jnp.concatenate([gathered(spread_ref, k, devices, params) for k in range(SLOTS)], axis=0)
    for p in range(params):
        own = jnp.dot(pick, blocks[:, p * cells : (p + 1) * cells], preferred_element_type=jnp.float32)
        own_ref[:, p * per_ray : (p + 1) * per_ray, :] = own.reshape(rays, per_ray, cells)

    lane = iota((per_ray, 128), 1)
    low = lane < bands
    pairs = per_ray * bands // 128
    mine = [iota((per_ray, 128), 0) == 2 * j + lane // bands for j in range(pairs)]

    def scales(rows):
        scale = []
        for half in range(params // 2):
            two = coefficient_ref[rows, half * 128 : half * 128 + 128]
            turned = pltpu.roll(two, bands, 1)
            scale.append(jnp.where(low, two, turned))
            scale.append(jnp.where(low, turned, two))
        return scale

    def rows_of(ray):
        return pl.ds(pl.multiple_of(ray * per_ray, per_ray), per_ray)

    def sense(ray):
        rows = rows_of(ray)
        sheet = held_ref[rows].reshape(per_ray * bands, cells)
        sensed = lax.dot_general(
            own_ref[ray].astype(jnp.bfloat16), sheet, (((1,), (1,)), ((), ())), preferred_element_type=jnp.float32
        )
        scale = scales(rows)
        total = jnp.zeros((per_ray, 128), jnp.float32)
        for j in range(pairs):
            part = scale[0] * sensed[:per_ray, j * 128 : (j + 1) * 128]
            for p in range(1, params):
                part += scale[p] * sensed[p * per_ray : (p + 1) * per_ray, j * 128 : (j + 1) * 128]
            total = jnp.where(mine[j], part, total)
        total_ref[rows, :] = total

    coefficient_copy.wait()

    def forward(g, carry):
        fetch(g).wait()
        for n in range(group):
            sense(g * group + n)
        return carry

    lax.fori_loop(0, chunks, forward, 0)

    predicted = total_ref[pl.ds(0, rays, stride=per_ray), :]
    for i in range(1, per_ray):
        predicted += total_ref[pl.ds(i, rays, stride=per_ray), :]
    predicted = predicted + pltpu.roll(predicted, bands, 1)
    observed_copy.wait()
    seen = observed_ref[...]
    seen = jnp.concatenate([seen, seen], axis=1)
    residual = jnp.where(iota((rays, 128), 0) < count_ref[0], predicted - seen, 0.0)
    residual_ref[...] = residual[:, :bands]
    twice_ref[...] = residual

    rows_all = params * per_ray
    keep = [
        (iota((rows_all, 128), 0) % per_ray == 2 * j + iota((rows_all, 128), 1) // bands)
        .astype(jnp.float32)
        .astype(jnp.bfloat16)
        for j in range(pairs)
    ]

    def adjoint(ray):
        rows = rows_of(ray)
        sheet = held_ref[rows].reshape(per_ray * bands, cells)
        residual = twice_ref[pl.ds(ray, 1), :]
        weight = jnp.concatenate([p * residual for p in scales(rows)], axis=0).astype(jnp.bfloat16)
        weight = jnp.concatenate([weight * keep[j] for j in range(pairs)], axis=1)
        grad_ref[ray] = jnp.dot(weight, sheet, preferred_element_type=jnp.float32)

    def backward(g, carry):
        for n in range(group):
            adjoint(g * group + n)
        return carry

    lax.fori_loop(0, chunks, backward, 0)

    grad = jnp.concatenate(
        [grad_ref[:, p * per_ray : (p + 1) * per_ray, :].reshape(hits, cells) for p in range(params)], axis=1
    ).astype(jnp.bfloat16)
    for k in range(SLOTS):
        place = slot == (iota((devices, hits), 0) + k * devices).astype(jnp.float32)
        place = place.astype(jnp.float32).astype(jnp.bfloat16)
        product = jnp.dot(place, grad, preferred_element_type=jnp.float32)
        spread(product, spread_ref, k, devices, params, cells)
    out_ref[...] = spread_ref[...].astype(jnp.bfloat16)


def sum_kernel(wanted_ref, returned_ref, out_hbm, spread_ref, out_ref, sems):
    params, tiles, cells = out_ref.shape
    devices = wanted_ref.shape[0]
    spread_ref[...] = returned_ref[...].astype(jnp.float32)
    across = wanted_ref[...].astype(jnp.float32).T
    picks = []
    for k in range(SLOTS):
        pick = across[k : k + 1, :] == (iota((tiles, devices), 0) + 1).astype(jnp.float32)
        picks.append(pick.astype(jnp.float32).astype(jnp.bfloat16))
    pick = jnp.concatenate(picks, axis=1)
    blocks = jnp.concatenate([gathered(spread_ref, k, devices, params) for k in range(SLOTS)], axis=0)
    for p in range(params):
        out_ref[p] = jnp.dot(pick, blocks[:, p * cells : (p + 1) * cells], preferred_element_type=jnp.float32)
        pltpu.make_async_copy(out_ref.at[p], out_hbm.at[p], sems.at[p]).start()
    for p in range(params):
        pltpu.make_async_copy(out_ref.at[p], out_hbm.at[p], sems.at[p]).wait()


def exchange(rows, devices, params, cells):
    sent = rows.reshape(devices, SLOTS, params, cells)
    back = lax.all_to_all(sent, AXES, split_axis=0, concat_axis=0, tiled=True)
    return back.reshape(devices * SLOTS * params, cells)


def per_device(kernel, coefficient, observed, ray_brick, tile_index, ray_count, earth_model):
    hits, bands, cells = kernel.shape
    params, tiles = earth_model.shape[1:3]
    rays = observed.shape[0]
    per_ray = hits // rays
    devices = lax.axis_size("lat") * lax.axis_size("dep")
    messages = devices * SLOTS * params
    f32, bf16 = jnp.float32, jnp.bfloat16
    shape = jax.ShapeDtypeStruct

    wanted, slot = pl.pallas_call(
        functools.partial(plan_kernel, per_ray=per_ray, devices=devices),
        out_shape=(shape((devices, 128), jnp.int32), shape((1, hits), f32)),
        in_specs=[SMEM, HBM, HBM],
        out_specs=(VMEM, VMEM),
        scratch_shapes=[
            pltpu.VMEM((1, hits), jnp.int32),
            pltpu.VMEM((1, hits), jnp.int32),
            pltpu.SemaphoreType.DMA((2,)),
        ],
        compiler_params=pltpu.CompilerParams(vmem_limit_bytes=8 * MIB),
        name="plan",
    )(ray_count, in_hbm(ray_brick.reshape(1, hits)), in_hbm(tile_index.reshape(1, hits)))
    requests = lax.all_to_all(wanted.reshape(devices, 1, 128), AXES, split_axis=0, concat_axis=0, tiled=True)
    requests = requests.reshape(devices, 128)
    model = pl.pallas_call(
        round_kernel,
        out_shape=shape((tiles, params * cells), bf16),
        in_specs=[VMEM],
        out_specs=VMEM,
        compiler_params=pltpu.CompilerParams(vmem_limit_bytes=8 * MIB),
        cost_estimate=pl.CostEstimate(flops=0, bytes_accessed=6 * tiles * params * cells, transcendentals=0),
        name="round",
    )(in_hbm(earth_model[0]))
    blocks = pl.pallas_call(
        functools.partial(fetch_kernel, params=params),
        out_shape=shape((messages, cells), bf16),
        in_specs=[VMEM, VMEM],
        out_specs=VMEM,
        scratch_shapes=[pltpu.VMEM((messages, cells), f32)],
        compiler_params=pltpu.CompilerParams(vmem_limit_bytes=16 * MIB),
        name="fetch",
    )(requests, model)
    arrived = exchange(blocks, devices, params, cells)
    group = 16
    residual, outgoing = pl.pallas_call(
        functools.partial(rays_kernel, per_ray=per_ray, params=params, group=group),
        out_shape=(shape((rays, bands), f32), shape((messages, cells), bf16)),
        in_specs=[SMEM, VMEM, VMEM, HBM, HBM, HBM],
        out_specs=(VMEM, VMEM),
        scratch_shapes=[
            pltpu.VMEM((hits, params * bands), f32),
            pltpu.VMEM((rays, bands), f32),
            pltpu.VMEM((messages, cells), f32),
            pltpu.VMEM((rays, params * per_ray, cells), f32),
            pltpu.VMEM((rays, params * per_ray, cells), f32),
            pltpu.VMEM((hits, 128), f32),
            pltpu.VMEM((rays, 128), f32),
            pltpu.VMEM((hits, bands, cells), bf16),
            pltpu.SemaphoreType.DMA((rays // group,)),
            pltpu.SemaphoreType.DMA((2,)),
        ],
        compiler_params=pltpu.CompilerParams(vmem_limit_bytes=28 * MIB),
        name="rays",
    )(ray_count, slot, arrived, in_hbm(coefficient), in_hbm(observed), in_hbm(kernel))
    returned = exchange(outgoing, devices, params, cells)
    gradient = pl.pallas_call(
        sum_kernel,
        out_shape=shape((params, tiles, cells), f32),
        in_specs=[VMEM, VMEM],
        out_specs=HBM,
        scratch_shapes=[
            pltpu.VMEM((messages, cells), f32),
            pltpu.VMEM((params, tiles, cells), f32),
            pltpu.SemaphoreType.DMA((params,)),
        ],
        compiler_params=pltpu.CompilerParams(vmem_limit_bytes=16 * MIB),
        name="add",
    )(requests, returned)
    return residual, gradient[None]


def solution(mesh):
    return jax.shard_map(
        per_device,
        mesh=mesh,
        in_specs=(
            P(AXES, None, None),
            P(AXES, None),
            P(AXES, None),
            P(AXES, None),
            P(AXES),
            P(AXES),
            P(AXES, None, None, None),
        ),
        out_specs=(P(AXES, None), P(AXES, None, None, None)),
        check_vma=False,
    )
```

time: 123 us -> 105 us (0.85)
  blocking collectives: 92.8 us -> 62.7 us
  starting transfers between devices: 0 us -> 15.7 us
  Pallas kernels: 28.5 us -> 13.6 us
  waiting for transfers between devices: 0 us -> 11.4 us
    all_to_all x1 -> x0, blocking collectives: 28.7 us -> none  [per_device(): lax.all_to_all(wanted.reshape(devices, 1, 128), AXES, split_axis=0, conca...]
    all_to_all x0 -> x1, starting transfers between devices: none -> 15.7 us  [per_device(): lax.all_to_all(wanted.reshape(devices, 1, 128), AXES, split_axis=0, conca...]
    pallas_call x1, Pallas kernels: 20.6 us -> 7.94 us  [per_device(): pl.pallas_call(functools.partial(rays_kernel, per_ray=per_ray, params=par...]
    all_to_all x0 -> x1, waiting for transfers between devices: none -> 11.4 us  [per_device(): lax.all_to_all(wanted.reshape(devices, 1, 128), AXES, split_axis=0, conca...]
    all_to_all x2, blocking collectives: 64.1 us -> 62.7 us  [exchange(): back = lax.all_to_all(sent, AXES, split_axis=0, concat_axis=0, tiled=True)]
    pallas_call x1, Pallas kernels: 3.27 us -> 1.92 us  [per_device(): pl.pallas_call(sum_kernel, out_shape=shape((params, tiles, cells), f32),...]
    pallas_call x1 -> x2, Pallas kernels: 2.86 us -> 1.97 us  [the longest x1 1.3 us: per_device(): pl.pallas_call(round_kernel, out_shape=shape((tiles, params * cells), bf1...]
  transfers between devices with their start and end apart: 0 -> 1, of which waited for: 0 -> 1; matrix products, arithmetic and copies ran while one was open for 0% -> 0% of each run, Pallas kernels for 0% -> 1%
where the time goes in v2:
time: 105 us
  blocking collectives  62.7 us (60%)
  starting transfers between devices  15.7 us (15%)
  Pallas kernels  13.6 us (13%)
  waiting for transfers between devices  11.4 us (11%)
  between operations  1.32 us (1%)
    all_to_all x2, blocking collectives, exchange(): back = lax.all_to_all(sent, AXES, split_axis=0, concat_axis=0, tiled=True)  62.7 us
    all_to_all x1, starting transfers between devices, per_device(): lax.all_to_all(wanted.reshape(devices, 1, 128), AXES, split_axis=0, conca...  15.7 us
    all_to_all x1, waiting for transfers between devices, per_device(): lax.all_to_all(wanted.reshape(devices, 1, 128), AXES, split_axis=0, conca...  11.4 us
    pallas_call x1, Pallas kernels, per_device(): pl.pallas_call(functools.partial(rays_kernel, per_ray=per_ray, params=par...  7.94 us
  transfers between devices with their start and end apart: 1, of which 1 were waited for; matrix products, arithmetic and copies ran while one was open for 0% of the time, Pallas kernels for 1%

profile of v2, /device:TPU:1, one launch (start us, length us, event | category | flops | bytes accessed | tf_op | source)
XLA Modules:
  0.0 104.6 jit_solution(13759606329481177812)
XLA Ops:
  1.3 1.8 %plan.1 = (s32[256,128]{1,0:T(8,128)}, f32[1,512]{1,0:T(1,128)S(1)}) custom-call(s32[1]{0:T(128)S(6)} %copy.10.count_ref, s32[1,512]{1,0:T(1,128)} %bitcast.20, s32[1,512]{1,0:T(1,128)} %bitcast.21), custom_call_target="tpu_custom_call" | custom-call | tf_op jit(solution)/shard_map/plan/pallas_call | solution.py:250
  3.1 15.7 %all-to-all-start = ((s32[256,1,128]{2,1,0:T(1,128)}), s32[256,1,128]{2,1,0:T(1,128)S(1)}, u32[]{:S(2)}, u32[]{:S(2)}) async-start(s32[256,1,128]{2,1,0:T(1,128)} %bitcast.3), calls=%async_computation | async-start | bytes 262144 | tf_op jit(solution)/shard_map/all_to_all | solution.py:263
  18.7 1.3 %round.1.model_ref = bf16[512,512]{1,0:T(8,128)(2,1)S(1)} custom-call(f32[4,512,128]{2,1,0:T(8,128)} %bitcast.18), custom_call_target="tpu_custom_call" | custom-call | bytes 1572864 | tf_op jit(solution)/shard_map/round/pallas_call | solution.py:265
  20.0 11.4 %all-to-all-done = s32[256,1,128]{2,1,0:T(1,128)S(1)} async-done(((s32[256,1,128]{2,1,0:T(1,128)}), s32[256,1,128]{2,1,0:T(1,128)S(1)}, u32[]{:S(2)}, u32[]{:S(2)}) %all-to-all-start) | async-done | bytes 131104 | tf_op jit(solution)/shard_map/all_to_all | solution.py:263
  31.4 0.7 fetch.1
  32.1 31.0 %all_to_all.15 = bf16[256,3,4,128]{3,2,1,0:T(4,128)(2,1)S(1)} all-to-all(bf16[256,3,4,128]{3,2,1,0:T(4,128)(2,1)S(1)} %bitcast.13), channel_id=1, replica_groups=mesh['lat'=64,'dep'=4] {'lat','dep'}, dimensions={0} | all-to-all | bytes 1572864 | tf_op jit(solution)/shard_map/all_to_all | solution.py:236
  63.0 7.9 %rays.1 = (f32[64,64]{1,0:T(8,128)}, bf16[3072,128]{1,0:T(8,128)(2,1)S(1)}) custom-call(s32[1]{0:T(128)S(6)} %copy.10.count_ref, f32[1,512]{1,0:T(1,128)S(1)} %get-tuple-element.6.slot_ref, bf16[3072,128]{1,0:T(8,128)(2,1)S(1)} %bitcast.14, f32[512,256]{1,0:T(8,128)} %coefficient_hbm.1, f32[64,64]{1,0:T(8,128)} %observed_hbm.1, bf16[512,64,128]{2,1,0:T(8,128)(2,1)} %kernel_ref.1), custom_call_target="tpu_custom_call" | custom-call | tf_op jit(solution)/shard_map/rays/pallas_call | solution.py:285
  71.0 31.7 %all_to_all.16 = bf16[256,3,4,128]{3,2,1,0:T(4,128)(2,1)S(1)} all-to-all(bf16[256,3,4,128]{3,2,1,0:T(4,128)(2,1)S(1)} %bitcast.17), channel_id=1, replica_groups=mesh['lat'=64,'dep'=4] {'lat','dep'}, dimensions={0} | all-to-all | bytes 1572864 | tf_op jit(solution)/shard_map/all_to_all | solution.py:236
  102.7 1.9 %add.1 = f32[4,512,128]{2,1,0:T(8,128)} custom-call(s32[256,128]{1,0:T(8,128)S(1)} %bitcast.16, bf16[3072,128]{1,0:T(8,128)(2,1)S(1)} %bitcast.12), custom_call_target="tpu_custom_call" | custom-call | tf_op jit(solution)/shard_map/add/pallas_call | solution.py:306
Async XLA Ops:
  3.1 28.3 %all-to-all-start = ((s32[256,1,128]{2,1,0:T(1,128)}), s32[256,1,128]{2,1,0:T(1,128)S(1)}, u32[]{:S(2)}, u32[]{:S(2)}) async-start(s32[256,1,128]{2,1,0:T(1,128)} %bitcast.3), calls=%async_computation | async-start | bytes 262144 | tf_op jit(solution)/shard_map/all_to_all | solution.py:263

commit v3 on v2

--- a/solution.py
+++ b/solution.py
@@ -29,12 +29,16 @@
 
 
 def plan_kernel(
-    count_ref, brick_hbm, tile_hbm, wanted_ref, slot_ref, brick_ref, tile_ref, sems, *, per_ray, devices
+    count_ref, brick_hbm, tile_hbm, model_hbm, wanted_ref, slot_ref, low_ref, brick_ref, tile_ref, model_ref, sems,
+    *, per_ray, devices,
 ):
     brick_copy = pltpu.make_async_copy(brick_hbm, brick_ref, sems.at[0])
     tile_copy = pltpu.make_async_copy(tile_hbm, tile_ref, sems.at[1])
     brick_copy.start()
     tile_copy.start()
+    params, _, cells = model_ref.shape
+    for p in range(params):
+        pltpu.make_async_copy(model_hbm.at[p], model_ref.at[p], sems.at[2 + p]).start()
     hits = brick_ref.shape[1]
     live = count_ref[0] * per_ray
     brick_copy.wait()
@@ -59,22 +63,21 @@
         hit = jnp.where(slot == owner + float(k * devices), tile, 0.0)
         wanted = jnp.where(lane == k, jnp.sum(hit, axis=1, keepdims=True), wanted)
     wanted_ref[...] = wanted.astype(jnp.int32)
-
-
-def spread(product, spread_ref, k, rows, params, cells):
     for p in range(params):
-        spread_ref[pl.ds(k * params + p, rows, stride=SLOTS * params), :] = product[:, p * cells : (p + 1) * cells]
+        pltpu.make_async_copy(model_hbm.at[p], model_ref.at[p], sems.at[2 + p]).wait()
+        low_ref[:, p * cells : (p + 1) * cells] = model_ref[p].astype(jnp.bfloat16)
+
+
+def spread(product, spread_ref, rows, params, cells):
+    for k in range(SLOTS):
+        for p in range(params):
+            part = product[k * rows : (k + 1) * rows, p * cells : (p + 1) * cells]
+            spread_ref[pl.ds(k * params + p, rows, stride=SLOTS * params), :] = part
 
 
 def gathered(spread_ref, k, rows, params):
     parts = [spread_ref[pl.ds(k * params + p, rows, stride=SLOTS * params), :] for p in range(params)]
     return jnp.concatenate(parts, axis=1).astype(jnp.bfloat16)
-
-
-def round_kernel(model_ref, low_ref):
-    params, _, cells = model_ref.shape
-    for p in range(params):
-        low_ref[:, p * cells : (p + 1) * cells] = model_ref[p].astype(jnp.bfloat16)
 
 
 def fetch_kernel(wanted_ref, model_ref, out_ref, spread_ref, *, params):
@@ -83,11 +86,12 @@
     devices = wanted_ref.shape[0]
     model = model_ref[...]
     wanted = wanted_ref[...]
+    picks = []
     for k in range(SLOTS):
         pick = wanted[:, k : k + 1] == iota((devices, tiles), 1) + 1
-        pick = pick.astype(jnp.float32).astype(jnp.bfloat16)
-        product = jnp.dot(pick, model, preferred_element_type=jnp.float32)
-        spread(product, spread_ref, k, devices, params, cells)
+        picks.append(pick.astype(jnp.float32).astype(jnp.bfloat16))
+    pick = jnp.concatenate(picks, axis=0)
+    spread(jnp.dot(pick, model, preferred_element_type=jnp.float32), spread_ref, devices, params, cells)
     out_ref[...] = spread_ref[...].astype(jnp.bfloat16)
 
 
@@ -122,9 +126,11 @@
         picks.append(pick.astype(jnp.float32).astype(jnp.bfloat16))
     pick = jnp.concatenate(picks, axis=1)
     blocks = jnp.concatenate([gathered(spread_ref, k, devices, params) for k in range(SLOTS)], axis=0)
-    for p in range(params):
-        own = jnp.dot(pick, blocks[:, p * cells : (p + 1) * cells], preferred_element_type=jnp.float32)
-        own_ref[:, p * per_ray : (p + 1) * per_ray, :] = own.reshape(rays, per_ray, cells)
+    for p in range(0, params, 2):
+        own = jnp.dot(pick, blocks[:, p * cells : (p + 2) * cells], preferred_element_type=jnp.float32)
+        for q in range(2):
+            part = own[:, q * cells : (q + 1) * cells].reshape(rays, per_ray, cells)
+            own_ref[:, (p + q) * per_ray : (p + q + 1) * per_ray, :] = part
 
     lane = iota((per_ray, 128), 1)
     low = lane < bands
@@ -195,21 +201,15 @@
         weight = jnp.concatenate([weight * keep[j] for j in range(pairs)], axis=1)
         grad_ref[ray] = jnp.dot(weight, sheet, preferred_element_type=jnp.float32)
 
-    def backward(g, carry):
-        for n in range(group):
-            adjoint(g * group + n)
-        return carry
-
-    lax.fori_loop(0, chunks, backward, 0)
+    for n in range(rays):
+        adjoint(n)
 
     grad = jnp.concatenate(
         [grad_ref[:, p * per_ray : (p + 1) * per_ray, :].reshape(hits, cells) for p in range(params)], axis=1
     ).astype(jnp.bfloat16)
-    for k in range(SLOTS):
-        place = slot == (iota((devices, hits), 0) + k * devices).astype(jnp.float32)
-        place = place.astype(jnp.float32).astype(jnp.bfloat16)
-        product = jnp.dot(place, grad, preferred_element_type=jnp.float32)
-        spread(product, spread_ref, k, devices, params, cells)
+    place = slot == iota((SLOTS * devices, hits), 0).astype(jnp.float32)
+    place = place.astype(jnp.float32).astype(jnp.bfloat16)
+    spread(jnp.dot(place, grad, preferred_element_type=jnp.float32), spread_ref, devices, params, cells)
     out_ref[...] = spread_ref[...].astype(jnp.bfloat16)
 
 
@@ -224,9 +224,11 @@
         picks.append(pick.astype(jnp.float32).astype(jnp.bfloat16))
     pick = jnp.concatenate(picks, axis=1)
     blocks = jnp.concatenate([gathered(spread_ref, k, devices, params) for k in range(SLOTS)], axis=0)
-    for p in range(params):
-        out_ref[p] = jnp.dot(pick, blocks[:, p * cells : (p + 1) * cells], preferred_element_type=jnp.float32)
-        pltpu.make_async_copy(out_ref.at[p], out_hbm.at[p], sems.at[p]).start()
+    for p in range(0, params, 2):
+        total = jnp.dot(pick, blocks[:, p * cells : (p + 2) * cells], preferred_element_type=jnp.float32)
+        for q in range(2):
+            out_ref[p + q] = total[:, q * cells : (q + 1) * cells]
+            pltpu.make_async_copy(out_ref.at[p + q], out_hbm.at[p + q], sems.at[p + q]).start()
     for p in range(params):
         pltpu.make_async_copy(out_ref.at[p], out_hbm.at[p], sems.at[p]).wait()
 
@@ -247,30 +249,26 @@
     f32, bf16 = jnp.float32, jnp.bfloat16
     shape = jax.ShapeDtypeStruct
 
-    wanted, slot = pl.pallas_call(
+    wanted, slot, model = pl.pallas_call(
         functools.partial(plan_kernel, per_ray=per_ray, devices=devices),
-        out_shape=(shape((devices, 128), jnp.int32), shape((1, hits), f32)),
-        in_specs=[SMEM, HBM, HBM],
-        out_specs=(VMEM, VMEM),
+        out_shape=(
+            shape((devices, 128), jnp.int32),
+            shape((1, hits), f32),
+            shape((tiles, params * cells), bf16),
+        ),
+        in_specs=[SMEM, HBM, HBM, HBM],
+        out_specs=(VMEM, VMEM, VMEM),
         scratch_shapes=[
             pltpu.VMEM((1, hits), jnp.int32),
             pltpu.VMEM((1, hits), jnp.int32),
-            pltpu.SemaphoreType.DMA((2,)),
+            pltpu.VMEM((params, tiles, cells), f32),
+            pltpu.SemaphoreType.DMA((2 + params,)),
         ],
         compiler_params=pltpu.CompilerParams(vmem_limit_bytes=8 * MIB),
         name="plan",
-    )(ray_count, in_hbm(ray_brick.reshape(1, hits)), in_hbm(tile_index.reshape(1, hits)))
+    )(ray_count, in_hbm(ray_brick.reshape(1, hits)), in_hbm(tile_index.reshape(1, hits)), in_hbm(earth_model[0]))
     requests = lax.all_to_all(wanted.reshape(devices, 1, 128), AXES, split_axis=0, concat_axis=0, tiled=True)
     requests = requests.reshape(devices, 128)
-    model = pl.pallas_call(
-        round_kernel,
-        out_shape=shape((tiles, params * cells), bf16),
-        in_specs=[VMEM],
-        out_specs=VMEM,
-        compiler_params=pltpu.CompilerParams(vmem_limit_bytes=8 * MIB),
-        cost_estimate=pl.CostEstimate(flops=0, bytes_accessed=6 * tiles * params * cells, transcendentals=0),
-        name="round",
-    )(in_hbm(earth_model[0]))
     blocks = pl.pallas_call(
         functools.partial(fetch_kernel, params=params),
         out_shape=shape((messages, cells), bf16),

time: 105 us -> 103 us (0.981)
  blocking collectives: 62.7 us -> 90.9 us
  starting transfers between devices: 15.7 us -> 0 us
  waiting for transfers between devices: 11.4 us -> 0 us
  Pallas kernels: 13.6 us -> 10.9 us
    all_to_all x0 -> x1, blocking collectives: none -> 28.2 us  [per_device(): lax.all_to_all(wanted.reshape(devices, 1, 128), AXES, split_axis=0, conca...]
    all_to_all x1 -> x0, starting transfers between devices: 15.7 us -> none  [per_device(): lax.all_to_all(wanted.reshape(devices, 1, 128), AXES, split_axis=0, conca...]
    all_to_all x1 -> x0, waiting for transfers between devices: 11.4 us -> none  [per_device(): lax.all_to_all(wanted.reshape(devices, 1, 128), AXES, split_axis=0, conca...]
    pallas_call x1 -> x0, Pallas kernels: 1.3 us -> none  [per_device(): pl.pallas_call(round_kernel, out_shape=shape((tiles, params * cells), bf1...]
  transfers between devices with their start and end apart: 1 -> 0, of which waited for: 1 -> 0; matrix products, arithmetic and copies ran while one was open for 0% -> 0% of each run, Pallas kernels for 1% -> 0%
where the time goes in v3:
time: 103 us
  blocking collectives  90.9 us (88%)
  Pallas kernels  10.9 us (11%)
  between operations  1.3 us (1%)
    all_to_all x2, blocking collectives, exchange(): back = lax.all_to_all(sent, AXES, split_axis=0, concat_axis=0, tiled=True)  62.7 us
    all_to_all x1, blocking collectives, per_device(): lax.all_to_all(wanted.reshape(devices, 1, 128), AXES, split_axis=0, conca...  28.2 us
    pallas_call x1, Pallas kernels, per_device(): pl.pallas_call(functools.partial(rays_kernel, per_ray=per_ray, params=par...  7.25 us

profile of v3, /device:TPU:1, one launch (start us, length us, event | category | flops | bytes accessed | tf_op | source)
XLA Modules:
  0.0 103.0 jit_solution(6615935958309249791)
XLA Ops:
  1.3 1.3 %plan.1 = (s32[256,128]{1,0:T(8,128)S(1)}, f32[1,512]{1,0:T(1,128)S(1)}, bf16[512,512]{1,0:T(8,128)(2,1)S(1)}) custom-call(s32[1]{0:T(128)S(6)} %copy.10.count_ref, s32[1,512]{1,0:T(1,128)} %bitcast.21, s32[1,512]{1,0:T(1,128)} %bitcast.22, f32[4,512,128]{2,1,0:T(8,128)} %bitcast.19), custom_call_target="tpu_custom_call" | custom-call | tf_op jit(solution)/shard_map/plan/pallas_call | solution.py:252
  2.6 28.2 %all_to_all.15 = s32[256,1,128]{2,1,0:T(1,128)S(1)} all-to-all(s32[256,1,128]{2,1,0:T(1,128)S(1)} %bitcast.18), channel_id=1, replica_groups=mesh['lat'=64,'dep'=4] {'lat','dep'}, dimensions={0} | all-to-all | bytes 262144 | tf_op jit(solution)/shard_map/all_to_all | solution.py:270
  30.8 0.7 fetch.1
  31.4 31.0 %all_to_all.16 = bf16[256,3,4,128]{3,2,1,0:T(4,128)(2,1)S(1)} all-to-all(bf16[256,3,4,128]{3,2,1,0:T(4,128)(2,1)S(1)} %bitcast.13), channel_id=1, replica_groups=mesh['lat'=64,'dep'=4] {'lat','dep'}, dimensions={0} | all-to-all | bytes 1572864 | tf_op jit(solution)/shard_map/all_to_all | solution.py:238
  62.4 7.3 %rays.1 = (f32[64,64]{1,0:T(8,128)}, bf16[3072,128]{1,0:T(8,128)(2,1)S(1)}) custom-call(s32[1]{0:T(128)S(6)} %copy.10.count_ref, f32[1,512]{1,0:T(1,128)S(1)} %get-tuple-element.7.slot_ref, bf16[3072,128]{1,0:T(8,128)(2,1)S(1)} %bitcast.14, f32[512,256]{1,0:T(8,128)} %coefficient_hbm.1, f32[64,64]{1,0:T(8,128)} %observed_hbm.1, bf16[512,64,128]{2,1,0:T(8,128)(2,1)} %kernel_ref.1), custom_call_target="tpu_custom_call" | custom-call | tf_op jit(solution)/shard_map/rays/pallas_call | solution.py:283
  69.7 31.7 %all_to_all.17 = bf16[256,3,4,128]{3,2,1,0:T(4,128)(2,1)S(1)} all-to-all(bf16[256,3,4,128]{3,2,1,0:T(4,128)(2,1)S(1)} %bitcast.17), channel_id=1, replica_groups=mesh['lat'=64,'dep'=4] {'lat','dep'}, dimensions={0} | all-to-all | bytes 1572864 | tf_op jit(solution)/shard_map/all_to_all | solution.py:238
  101.4 1.7 %add.1 = f32[4,512,128]{2,1,0:T(8,128)} custom-call(s32[256,128]{1,0:T(8,128)S(1)} %bitcast.16, bf16[3072,128]{1,0:T(8,128)(2,1)S(1)} %bitcast.12), custom_call_target="tpu_custom_call" | custom-call | tf_op jit(solution)/shard_map/add/pallas_call | solution.py:304

commit v4 on v3

--- a/solution.py
+++ b/solution.py
@@ -9,7 +9,9 @@
 
 SLOTS = 3
 MIB = 1 << 20
-AXES = ("lat", "dep")
+AXES = ("zx", "core", "dep")
+GROUP = ("zx", "dep")
+ORDER = ("core", "zx", "dep")
 VMEM = pl.BlockSpec(memory_space=pltpu.VMEM)
 SMEM = pl.BlockSpec(memory_space=pltpu.SMEM)
 HBM = pl.BlockSpec(memory_space=pltpu.HBM)
@@ -29,8 +31,8 @@
 
 
 def plan_kernel(
-    count_ref, brick_hbm, tile_hbm, model_hbm, wanted_ref, slot_ref, low_ref, brick_ref, tile_ref, model_ref, sems,
-    *, per_ray, devices,
+    count_ref, brick_hbm, tile_hbm, model_hbm, wanted_ref, near_ref, far_ref, low_ref, brick_ref, tile_ref, model_ref, sems,
+    *, per_ray, members, depth,
 ):
     brick_copy = pltpu.make_async_copy(brick_hbm, brick_ref, sems.at[0])
     tile_copy = pltpu.make_async_copy(tile_hbm, tile_ref, sems.at[1])
@@ -43,7 +45,8 @@
     live = count_ref[0] * per_ray
     brick_copy.wait()
     tile_copy.wait()
-    brick = brick_ref[...].astype(jnp.float32)
+    named = brick_ref[...]
+    brick = named.astype(jnp.float32)
     down = column_of(brick)
     ranks = []
     for start in range(0, hits, 128):
@@ -52,15 +55,19 @@
         earlier = (down == across) & (first < iota((hits, 128), 1) + start) & (first < live)
         ranks.append(jnp.sum(earlier.astype(jnp.float32), axis=0, keepdims=True))
     rank = jnp.concatenate(ranks, axis=1)
+    core = lax.rem(lax.div(named, depth), 2)
+    member = lax.div(named, 2 * depth) * depth + lax.rem(named, depth)
+    core, member = core.astype(jnp.float32), member.astype(jnp.float32)
     alive = iota((1, hits), 1) < live
-    slot = jnp.where(alive, rank * devices + brick, -1.0)
-    slot_ref[...] = slot
+    near = jnp.where(alive, (core * SLOTS + rank) * members + member, -1.0)
+    near_ref[...] = near
+    far_ref[...] = jnp.where(alive, (rank * 2 + core) * members + member, -1.0)
     tile = tile_ref[...].astype(jnp.float32) + 1.0
-    owner = iota((devices, 1), 0).astype(jnp.float32)
-    lane = iota((devices, 128), 1)
-    wanted = jnp.zeros((devices, 128), jnp.float32)
-    for k in range(SLOTS):
-        hit = jnp.where(slot == owner + float(k * devices), tile, 0.0)
+    owner = iota((members, 1), 0).astype(jnp.float32)
+    lane = iota((members, 128), 1)
+    wanted = jnp.zeros((members, 128), jnp.float32)
+    for k in range(2 * SLOTS):
+        hit = jnp.where(near == owner + float(k * members), tile, 0.0)
         wanted = jnp.where(lane == k, jnp.sum(hit, axis=1, keepdims=True), wanted)
     wanted_ref[...] = wanted.astype(jnp.int32)
     for p in range(params):
@@ -68,39 +75,46 @@
         low_ref[:, p * cells : (p + 1) * cells] = model_ref[p].astype(jnp.bfloat16)
 
 
-def spread(product, spread_ref, rows, params, cells):
-    for k in range(SLOTS):
+def spread(product, spread_ref, first, slots, rows, params, cells):
+    for k in range(product.shape[0] // rows):
         for p in range(params):
             part = product[k * rows : (k + 1) * rows, p * cells : (p + 1) * cells]
-            spread_ref[pl.ds(k * params + p, rows, stride=SLOTS * params), :] = part
-
-
-def gathered(spread_ref, k, rows, params):
-    parts = [spread_ref[pl.ds(k * params + p, rows, stride=SLOTS * params), :] for p in range(params)]
-    return jnp.concatenate(parts, axis=1).astype(jnp.bfloat16)
-
-
-def fetch_kernel(wanted_ref, model_ref, out_ref, spread_ref, *, params):
-    tiles = model_ref.shape[0]
-    cells = model_ref.shape[1] // params
-    devices = wanted_ref.shape[0]
-    model = model_ref[...]
+            spread_ref[pl.ds((first + k) * params + p, rows, stride=slots * params), :] = part
+
+
+def gathered(spread_ref, slots, rows, params):
+    blocks = []
+    for k in range(slots):
+        parts = [spread_ref[pl.ds(k * params + p, rows, stride=slots * params), :] for p in range(params)]
+        blocks.append(jnp.concatenate(parts, axis=1).astype(jnp.bfloat16))
+    return jnp.concatenate(blocks, axis=0)
+
+
+def fetch_kernel(wanted_ref, own_ref, other_ref, out_ref, spread_ref, *, params):
+    tiles = own_ref.shape[0]
+    cells = own_ref.shape[1] // params
+    members = wanted_ref.shape[0]
+    even = lax.axis_index("core") == 0
+    own, other = own_ref[...], other_ref[...]
     wanted = wanted_ref[...]
-    picks = []
-    for k in range(SLOTS):
-        pick = wanted[:, k : k + 1] == iota((devices, tiles), 1) + 1
-        picks.append(pick.astype(jnp.float32).astype(jnp.bfloat16))
-    pick = jnp.concatenate(picks, axis=0)
-    spread(jnp.dot(pick, model, preferred_element_type=jnp.float32), spread_ref, devices, params, cells)
+    for core in range(2):
+        model = jnp.where(even, own, other) if core == 0 else jnp.where(even, other, own)
+        picks = []
+        for k in range(core * SLOTS, (core + 1) * SLOTS):
+            pick = wanted[:, k : k + 1] == iota((members, tiles), 1) + 1
+            picks.append(pick.astype(jnp.float32).astype(jnp.bfloat16))
+        product = jnp.dot(jnp.concatenate(picks, axis=0), model, preferred_element_type=jnp.float32)
+        spread(product, spread_ref, core * SLOTS, 2 * SLOTS, members, params, cells)
     out_ref[...] = spread_ref[...].astype(jnp.bfloat16)
 
 
 def rays_kernel(
-    count_ref, slot_ref, arrived_ref, coefficient_hbm, observed_hbm, kernel_ref,
+    count_ref, near_ref, far_ref, early_ref, arrived_ref, coefficient_hbm, observed_hbm, kernel_ref,
     residual_ref, out_ref, coefficient_ref, observed_ref, spread_ref, own_ref, grad_ref, total_ref, twice_ref,
     held_ref, sems, small_sems,
     *, per_ray, params, group,
 ):
+    del early_ref
     hits, bands, cells = held_ref.shape
     rays = observed_ref.shape[0]
     devices = arrived_ref.shape[0] // (SLOTS * params)
@@ -118,14 +132,13 @@
         fetch(i).start()
     observed_copy.start()
     spread_ref[...] = arrived_ref[...].astype(jnp.float32)
-    slot = slot_ref[...]
-    slot_down = column_of(slot)
+    slot_down = column_of(near_ref[...])
     picks = []
     for start in range(0, SLOTS * devices, 128):
         pick = slot_down == (iota((hits, 128), 1) + start).astype(jnp.float32)
         picks.append(pick.astype(jnp.float32).astype(jnp.bfloat16))
     pick = jnp.concatenate(picks, axis=1)
-    blocks = jnp.concatenate([gathered(spread_ref, k, devices, params) for k in range(SLOTS)], axis=0)
+    blocks = gathered(spread_ref, 2 * SLOTS, devices // 2, params)
     for p in range(0, params, 2):
         own = jnp.dot(pick, blocks[:, p * cells : (p + 2) * cells], preferred_element_type=jnp.float32)
         for q in range(2):
@@ -207,23 +220,29 @@
     grad = jnp.concatenate(
         [grad_ref[:, p * per_ray : (p + 1) * per_ray, :].reshape(hits, cells) for p in range(params)], axis=1
     ).astype(jnp.bfloat16)
-    place = slot == iota((SLOTS * devices, hits), 0).astype(jnp.float32)
+    place = far_ref[...] == iota((SLOTS * devices, hits), 0).astype(jnp.float32)
     place = place.astype(jnp.float32).astype(jnp.bfloat16)
-    spread(jnp.dot(place, grad, preferred_element_type=jnp.float32), spread_ref, devices, params, cells)
+    product = jnp.dot(place, grad, preferred_element_type=jnp.float32)
+    spread(product, spread_ref, 0, SLOTS, devices, params, cells)
     out_ref[...] = spread_ref[...].astype(jnp.bfloat16)
 
 
-def sum_kernel(wanted_ref, returned_ref, out_hbm, spread_ref, out_ref, sems):
+def sum_kernel(mine_ref, other_ref, returned_ref, out_hbm, spread_ref, out_ref, sems):
     params, tiles, cells = out_ref.shape
-    devices = wanted_ref.shape[0]
+    members = mine_ref.shape[0]
     spread_ref[...] = returned_ref[...].astype(jnp.float32)
-    across = wanted_ref[...].astype(jnp.float32).T
+    even = lax.axis_index("core") == 0
+    mine = mine_ref[...].astype(jnp.float32)
+    other = other_ref[...].astype(jnp.float32)
+    asked = [jnp.where(even, mine, other).T, jnp.where(even, other, mine).T]
     picks = []
     for k in range(SLOTS):
-        pick = across[k : k + 1, :] == (iota((tiles, devices), 0) + 1).astype(jnp.float32)
-        picks.append(pick.astype(jnp.float32).astype(jnp.bfloat16))
+        for rows in asked:
+            row = jnp.where(even, rows[k : k + 1], rows[SLOTS + k : SLOTS + k + 1])
+            pick = row == (iota((tiles, members), 0) + 1).astype(jnp.float32)
+            picks.append(pick.astype(jnp.float32).astype(jnp.bfloat16))
     pick = jnp.concatenate(picks, axis=1)
-    blocks = jnp.concatenate([gathered(spread_ref, k, devices, params) for k in range(SLOTS)], axis=0)
+    blocks = gathered(spread_ref, SLOTS, 2 * members, params)
     for p in range(0, params, 2):
         total = jnp.dot(pick, blocks[:, p * cells : (p + 2) * cells], preferred_element_type=jnp.float32)
         for q in range(2):
@@ -233,10 +252,11 @@
         pltpu.make_async_copy(out_ref.at[p], out_hbm.at[p], sems.at[p]).wait()
 
 
-def exchange(rows, devices, params, cells):
-    sent = rows.reshape(devices, SLOTS, params, cells)
-    back = lax.all_to_all(sent, AXES, split_axis=0, concat_axis=0, tiled=True)
-    return back.reshape(devices * SLOTS * params, cells)
+def exchange(rows, axes, devices, params, cells):
+    slots = rows.shape[0] // (devices * params)
+    sent = rows.reshape(devices, slots, params, cells)
+    back = lax.all_to_all(sent, axes, split_axis=0, concat_axis=0, tiled=True)
+    return back.reshape(devices * slots * params, cells)
 
 
 def per_device(kernel, coefficient, observed, ray_brick, tile_index, ray_count, earth_model):
@@ -244,20 +264,24 @@
     params, tiles = earth_model.shape[1:3]
     rays = observed.shape[0]
     per_ray = hits // rays
-    devices = lax.axis_size("lat") * lax.axis_size("dep")
+    depth = lax.axis_size("dep")
+    members = lax.axis_size("zx") * depth
+    devices = 2 * members
+    swap = [(0, 1), (1, 0)]
     messages = devices * SLOTS * params
     f32, bf16 = jnp.float32, jnp.bfloat16
     shape = jax.ShapeDtypeStruct
 
-    wanted, slot, model = pl.pallas_call(
-        functools.partial(plan_kernel, per_ray=per_ray, devices=devices),
+    wanted, near, far, model = pl.pallas_call(
+        functools.partial(plan_kernel, per_ray=per_ray, members=members, depth=depth),
         out_shape=(
-            shape((devices, 128), jnp.int32),
+            shape((members, 128), jnp.int32),
+            shape((1, hits), f32),
             shape((1, hits), f32),
             shape((tiles, params * cells), bf16),
         ),
         in_specs=[SMEM, HBM, HBM, HBM],
-        out_specs=(VMEM, VMEM, VMEM),
+        out_specs=(VMEM, VMEM, VMEM, VMEM),
         scratch_shapes=[
             pltpu.VMEM((1, hits), jnp.int32),
             pltpu.VMEM((1, hits), jnp.int32),
@@ -267,23 +291,25 @@
         compiler_params=pltpu.CompilerParams(vmem_limit_bytes=8 * MIB),
         name="plan",
     )(ray_count, in_hbm(ray_brick.reshape(1, hits)), in_hbm(tile_index.reshape(1, hits)), in_hbm(earth_model[0]))
-    requests = lax.all_to_all(wanted.reshape(devices, 1, 128), AXES, split_axis=0, concat_axis=0, tiled=True)
-    requests = requests.reshape(devices, 128)
+    other_model = lax.ppermute(model, "core", swap)
+    requests = lax.all_to_all(wanted.reshape(members, 1, 128), GROUP, split_axis=0, concat_axis=0, tiled=True)
+    requests = requests.reshape(members, 128)
+    other_requests = lax.ppermute(requests, "core", swap)
     blocks = pl.pallas_call(
         functools.partial(fetch_kernel, params=params),
         out_shape=shape((messages, cells), bf16),
-        in_specs=[VMEM, VMEM],
+        in_specs=[VMEM, VMEM, VMEM],
         out_specs=VMEM,
         scratch_shapes=[pltpu.VMEM((messages, cells), f32)],
         compiler_params=pltpu.CompilerParams(vmem_limit_bytes=16 * MIB),
         name="fetch",
-    )(requests, model)
-    arrived = exchange(blocks, devices, params, cells)
+    )(requests, model, other_model)
+    arrived = exchange(blocks, GROUP, members, params, cells)
     group = 16
     residual, outgoing = pl.pallas_call(
         functools.partial(rays_kernel, per_ray=per_ray, params=params, group=group),
         out_shape=(shape((rays, bands), f32), shape((messages, cells), bf16)),
-        in_specs=[SMEM, VMEM, VMEM, HBM, HBM, HBM],
+        in_specs=[SMEM, VMEM, VMEM, VMEM, VMEM, HBM, HBM, HBM],
         out_specs=(VMEM, VMEM),
         scratch_shapes=[
             pltpu.VMEM((hits, params * bands), f32),
@@ -299,12 +325,12 @@
         ],
         compiler_params=pltpu.CompilerParams(vmem_limit_bytes=28 * MIB),
         name="rays",
-    )(ray_count, slot, arrived, in_hbm(coefficient), in_hbm(observed), in_hbm(kernel))
-    returned = exchange(outgoing, devices, params, cells)
+    )(ray_count, near, far, other_requests, arrived, in_hbm(coefficient), in_hbm(observed), in_hbm(kernel))
+    returned = exchange(outgoing, ORDER, devices, params, cells)
     gradient = pl.pallas_call(
         sum_kernel,
         out_shape=shape((params, tiles, cells), f32),
-        in_specs=[VMEM, VMEM],
+        in_specs=[VMEM, VMEM, VMEM],
         out_specs=HBM,
         scratch_shapes=[
             pltpu.VMEM((messages, cells), f32),
@@ -313,14 +339,16 @@
         ],
         compiler_params=pltpu.CompilerParams(vmem_limit_bytes=16 * MIB),
         name="add",
-    )(requests, returned)
+    )(requests, other_requests, returned)
     return residual, gradient[None]
 
 
 def solution(mesh):
+    lat, dep = mesh.devices.shape
+    chips = jax.sharding.Mesh(mesh.devices.reshape(lat // 2, 2, dep), AXES)
     return jax.shard_map(
         per_device,
-        mesh=mesh,
+        mesh=chips,
         in_specs=(
             P(AXES, None, None),
             P(AXES, None),

time: 103 us -> 105 us (1.019)
  blocking collectives: 90.9 us -> 58.8 us
  waiting for transfers between devices: 0 us -> 21.5 us
  starting transfers between devices: 0 us -> 11 us
  Pallas kernels: 10.9 us -> 12.4 us
    all_to_all x3 -> x2, blocking collectives: 90.9 us -> 58.8 us  [the longest x1 34.4 us: exchange(): back = lax.all_to_all(sent, axes, split_axis=0, concat_axis=0, tiled=True)]
    all_to_all x0 -> x1, waiting for transfers between devices: none -> 20.6 us  [exchange(): back = lax.all_to_all(sent, axes, split_axis=0, concat_axis=0, tiled=True)]
    all_to_all x0 -> x1, starting transfers between devices: none -> 6.18 us  [exchange(): back = lax.all_to_all(sent, axes, split_axis=0, concat_axis=0, tiled=True)]
    ppermute x0 -> x2, starting transfers between devices: none -> 4.81 us  [the longest x1 3.29 us: per_device(): other_model = lax.ppermute(model, 'core', swap)]
  transfers between devices with their start and end apart: 0 -> 3, of which waited for: 0 -> 2; matrix products, arithmetic and copies ran while one was open for 0% -> 0% of each run, Pallas kernels for 0% -> 0%
where the time goes in v4:
time: 105 us
  blocking collectives  58.8 us (56%)
  waiting for transfers between devices  21.5 us (20%)
  Pallas kernels  12.4 us (12%)
  starting transfers between devices  11 us (10%)
  between operations  1.31 us (1%)
    all_to_all x1, blocking collectives, exchange(): back = lax.all_to_all(sent, axes, split_axis=0, concat_axis=0, tiled=True)  34.4 us
    all_to_all x1, blocking collectives, per_device(): lax.all_to_all(wanted.reshape(members, 1, 128), GROUP, split_axis=0, conc...  24.4 us
    all_to_all x1, waiting for transfers between devices, exchange(): back = lax.all_to_all(sent, axes, split_axis=0, concat_axis=0, tiled=True)  20.6 us
    pallas_call x1, Pallas kernels, per_device(): pl.pallas_call(functools.partial(rays_kernel, per_ray=per_ray, params=par...  7.78 us
    all_to_all x1, starting transfers between devices, exchange(): back = lax.all_to_all(sent, axes, split_axis=0, concat_axis=0, tiled=True)  6.18 us
    ppermute x1, starting transfers between devices, per_device(): other_model = lax.ppermute(model, 'core', swap)  3.29 us
  transfers between devices with their start and end apart: 3, of which 2 were waited for; matrix products, arithmetic and copies ran while one was open for 0% of the time, Pallas kernels for 0%

profile of v4, /device:TPU:1, one launch (start us, length us, event | category | flops | bytes accessed | tf_op | source)
XLA Modules:
  0.0 104.9 jit_solution(5280351314635785587)
XLA Ops:
  1.3 1.3 %plan.1 = (s32[128,128]{1,0:T(8,128)S(1)}, f32[1,512]{1,0:T(1,128)S(1)}, f32[1,512]{1,0:T(1,128)S(1)}, bf16[512,512]{1,0:T(8,128)(2,1)S(1)}) custom-call(s32[1]{0:T(128)S(6)} %copy.10.count_ref, s32[1,512]{1,0:T(1,128)} %bitcast.21, s32[1,512]{1,0:T(1,128)} %bitcast.22, f32[4,512,128]{2,1,0:T(8,128)} %bitcast.19), custom_call_target="tpu_custom_call" | custom-call | tf_op jit(solution)/shard_map/plan/pallas_call | solution.py:275
  2.6 3.3 %collective-permute-start.1 = (bf16[512,512]{1,0:T(8,128)(2,1)S(1)}, bf16[512,512]{1,0:T(8,128)(2,1)S(1)}, u32[]{:S(2)}, u32[]{:S(2)}) collective-permute-start(bf16[512,512]{1,0:T(8,128)(2,1)S(1)} %get-tuple-element.11.own_ref), channel_id=1, source_target_pairs={{0,4},{4,0},{1,5},{5,1},{2,6},{6,2},{3,7},{7,3},{8,12},{12,8},{9,1... | collective-permute-start | bytes 1572872 | tf_op jit(solution)/shard_map/ppermute | solution.py:294
  5.9 24.4 %all_to_all.15 = s32[128,1,128]{2,1,0:T(1,128)S(1)} all-to-all(s32[128,1,128]{2,1,0:T(1,128)S(1)} %bitcast.18), channel_id=1, replica_groups=mesh['zx'=32,'core'=2,'dep'=4] {'zx','dep'}, dimensions={0} | all-to-all | bytes 131072 | tf_op jit(solution)/shard_map/all_to_all | solution.py:295
  30.2 0.0 collective-permute-done.1.other_ref
  30.2 1.6 %fetch.1 = bf16[3072,128]{1,0:T(8,128)(2,1)} custom-call(s32[128,128]{1,0:T(8,128)S(1)} %bitcast.15, bf16[512,512]{1,0:T(8,128)(2,1)S(1)} %get-tuple-element.11.own_ref, bf16[512,512]{1,0:T(8,128)(2,1)S(1)} %collective-permute-done.1.other_ref), custom_call_target="tpu_custom_call" | custom-call | tf_op jit(solution)/shard_map/fetch/pallas_call | solution.py:298
  31.9 6.2 %all-to-all-start.1 = ((bf16[128,6,4,128]{3,2,1,0:T(4,128)(2,1)}), bf16[128,6,4,128]{3,2,1,0:T(4,128)(2,1)S(1)}, u32[]{:S(2)}, u32[]{:S(2)}) async-start(bf16[128,6,4,128]{3,2,1,0:T(4,128)(2,1)} %bitcast.6), calls=%async_computation.1 | async-start | bytes 1572864 | tf_op jit(solution)/shard_map/all_to_all | solution.py:258
  38.1 1.5 %collective-permute-start = (s32[128,128]{1,0:T(8,128)S(1)}, s32[128,128]{1,0:T(8,128)S(1)}, u32[]{:S(2)}, u32[]{:S(2)}) collective-permute-start(s32[128,128]{1,0:T(8,128)S(1)} %bitcast.16), channel_id=1, source_target_pairs={{0,4},{4,0},{1,5},{5,1},{2,6},{6,2},{3,7},{7,3},{8,12},{12,8},{9,1... | collective-permute-start | bytes 196616 | tf_op jit(solution)/shard_map/ppermute | solution.py:297
  39.6 0.9 collective-permute-done.early_ref.other_ref
  40.5 20.6 %all-to-all-done.1 = bf16[128,6,4,128]{3,2,1,0:T(4,128)(2,1)S(1)} async-done(((bf16[128,6,4,128]{3,2,1,0:T(4,128)(2,1)}), bf16[128,6,4,128]{3,2,1,0:T(4,128)(2,1)S(1)}, u32[]{:S(2)}, u32[]{:S(2)}) %all-to-all-start.1) | async-done | bytes 786464 | tf_op jit(solution)/shard_map/all_to_all | solution.py:258
  61.1 7.8 %rays.1 = (f32[64,64]{1,0:T(8,128)}, bf16[3072,128]{1,0:T(8,128)(2,1)S(1)}) custom-call(s32[1]{0:T(128)S(6)} %copy.10.count_ref, f32[1,512]{1,0:T(1,128)S(1)} %get-tuple-element.8.near_ref, f32[1,512]{1,0:T(1,128)S(1)} %get-tuple-element.9.far_ref, s32[128,128]{1,0:T(8,128)S(1)} %collective-permute-done.early_ref.other_ref, bf16[3072,128]{1,0:T(8,128)(2,1)S(1)} %bitcast.12, ...), custom_call_target="tpu_custom_call" | custom-call | tf_op jit(solution)/shard_map/rays/pallas_call | solution.py:309
  68.9 34.4 %all_to_all.16 = bf16[256,3,4,128]{3,2,1,0:T(4,128)(2,1)S(1)} all-to-all(bf16[256,3,4,128]{3,2,1,0:T(4,128)(2,1)S(1)} %bitcast.14), channel_id=1, replica_groups=mesh['zx'=32,'core'=2,'dep'=4] {'core','zx','dep'}, dimensions={0} | all-to-all | bytes 1572864 | tf_op jit(solution)/shard_map/all_to_all | solution.py:258
  103.3 1.7 %add.1 = f32[4,512,128]{2,1,0:T(8,128)} custom-call(s32[128,128]{1,0:T(8,128)S(1)} %bitcast.17, s32[128,128]{1,0:T(8,128)S(1)} %collective-permute-done.early_ref.other_ref, bf16[3072,128]{1,0:T(8,128)(2,1)S(1)} %bitcast.13), custom_call_target="tpu_custom_call" | custom-call | tf_op jit(solution)/shard_map/add/pallas_call | solution.py:330
Async XLA Ops:
  2.6 27.7 %collective-permute-start.1 = (bf16[512,512]{1,0:T(8,128)(2,1)S(1)}, bf16[512,512]{1,0:T(8,128)(2,1)S(1)}, u32[]{:S(2)}, u32[]{:S(2)}) collective-permute-start(bf16[512,512]{1,0:T(8,128)(2,1)S(1)} %get-tuple-element.11.own_ref), channel_id=1, source_target_pairs={{0,4},{4,0},{1,5},{5,1},{2,6},{6,2},{3,7},{7,3},{8,12},{12,8},{9,1... | collective-permute-start | bytes 1572872 | tf_op jit(solution)/shard_map/ppermute | solution.py:294
  31.9 29.2 %all-to-all-start.1 = ((bf16[128,6,4,128]{3,2,1,0:T(4,128)(2,1)}), bf16[128,6,4,128]{3,2,1,0:T(4,128)(2,1)S(1)}, u32[]{:S(2)}, u32[]{:S(2)}) async-start(bf16[128,6,4,128]{3,2,1,0:T(4,128)(2,1)} %bitcast.6), calls=%async_computation.1 | async-start | bytes 1572864 | tf_op jit(solution)/shard_map/all_to_all | solution.py:258
  38.1 2.4 %collective-permute-start = (s32[128,128]{1,0:T(8,128)S(1)}, s32[128,128]{1,0:T(8,128)S(1)}, u32[]{:S(2)}, u32[]{:S(2)}) collective-permute-start(s32[128,128]{1,0:T(8,128)S(1)} %bitcast.16), channel_id=1, source_target_pairs={{0,4},{4,0},{1,5},{5,1},{2,6},{6,2},{3,7},{7,3},{8,12},{12,8},{9,1... | collective-permute-start | bytes 196616 | tf_op jit(solution)/shard_map/ppermute | solution.py:297

commit v5 on v3

--- a/solution.py
+++ b/solution.py
@@ -149,26 +149,34 @@
     def rows_of(ray):
         return pl.ds(pl.multiple_of(ray * per_ray, per_ray), per_ray)
 
-    def sense(ray):
-        rows = rows_of(ray)
-        sheet = held_ref[rows].reshape(per_ray * bands, cells)
-        sensed = lax.dot_general(
-            own_ref[ray].astype(jnp.bfloat16), sheet, (((1,), (1,)), ((), ())), preferred_element_type=jnp.float32
+    blank = jnp.zeros((params * per_ray, cells), jnp.bfloat16)
+
+    def sense(first):
+        rows = pl.ds(pl.multiple_of(first * per_ray, 2 * per_ray), 2 * per_ray)
+        sheet = held_ref[rows].reshape(2, per_ray * bands, cells)
+        sheet = jnp.concatenate([sheet[0], sheet[1]], axis=1)
+        block = own_ref[pl.ds(first, 2)].astype(jnp.bfloat16)
+        block = jnp.concatenate(
+            [jnp.concatenate([block[0], blank], axis=1), jnp.concatenate([blank, block[1]], axis=1)], axis=0
         )
-        scale = scales(rows)
-        total = jnp.zeros((per_ray, 128), jnp.float32)
-        for j in range(pairs):
-            part = scale[0] * sensed[:per_ray, j * 128 : (j + 1) * 128]
-            for p in range(1, params):
-                part += scale[p] * sensed[p * per_ray : (p + 1) * per_ray, j * 128 : (j + 1) * 128]
-            total = jnp.where(mine[j], part, total)
-        total_ref[rows, :] = total
+        both = lax.dot_general(block, sheet, (((1,), (1,)), ((), ())), preferred_element_type=jnp.float32)
+        for n in range(2):
+            sensed = both[n * params * per_ray : (n + 1) * params * per_ray]
+            rows = rows_of(first + n)
+            scale = scales(rows)
+            total = jnp.zeros((per_ray, 128), jnp.float32)
+            for j in range(pairs):
+                part = scale[0] * sensed[:per_ray, j * 128 : (j + 1) * 128]
+                for p in range(1, params):
+                    part += scale[p] * sensed[p * per_ray : (p + 1) * per_ray, j * 128 : (j + 1) * 128]
+                total = jnp.where(mine[j], part, total)
+            total_ref[rows, :] = total
 
     coefficient_copy.wait()
 
     def forward(g, carry):
         fetch(g).wait()
-        for n in range(group):
+        for n in range(0, group, 2):
             sense(g * group + n)
         return carry
 

time: 103 us -> 103 us (level)
  no operation moved by 1% of the time
where the time goes in v5:
time: 103 us
  blocking collectives  90.9 us (88%)
  Pallas kernels  10.6 us (10%)
  between operations  1.3 us (1%)
    all_to_all x2, blocking collectives, exchange(): back = lax.all_to_all(sent, AXES, split_axis=0, concat_axis=0, tiled=True)  62.7 us
    all_to_all x1, blocking collectives, per_device(): lax.all_to_all(wanted.reshape(devices, 1, 128), AXES, split_axis=0, conca...  28.2 us
    pallas_call x1, Pallas kernels, per_device(): pl.pallas_call(functools.partial(rays_kernel, per_ray=per_ray, params=par...  6.99 us

profile of v5, /device:TPU:1, one launch (start us, length us, event | category | flops | bytes accessed | tf_op | source)
XLA Modules:
  0.0 102.8 jit_solution(5923850251365581412)
XLA Ops:
  1.3 1.3 %plan.1 = (s32[256,128]{1,0:T(8,128)S(1)}, f32[1,512]{1,0:T(1,128)S(1)}, bf16[512,512]{1,0:T(8,128)(2,1)S(1)}) custom-call(s32[1]{0:T(128)S(6)} %copy.10.count_ref, s32[1,512]{1,0:T(1,128)} %bitcast.21, s32[1,512]{1,0:T(1,128)} %bitcast.22, f32[4,512,128]{2,1,0:T(8,128)} %bitcast.19), custom_call_target="tpu_custom_call" | custom-call | tf_op jit(solution)/shard_map/plan/pallas_call | solution.py:260
  2.6 28.2 %all_to_all.15 = s32[256,1,128]{2,1,0:T(1,128)S(1)} all-to-all(s32[256,1,128]{2,1,0:T(1,128)S(1)} %bitcast.18), channel_id=1, replica_groups=mesh['lat'=64,'dep'=4] {'lat','dep'}, dimensions={0} | all-to-all | bytes 262144 | tf_op jit(solution)/shard_map/all_to_all | solution.py:278
  30.8 0.7 fetch.1
  31.4 31.0 %all_to_all.16 = bf16[256,3,4,128]{3,2,1,0:T(4,128)(2,1)S(1)} all-to-all(bf16[256,3,4,128]{3,2,1,0:T(4,128)(2,1)S(1)} %bitcast.13), channel_id=1, replica_groups=mesh['lat'=64,'dep'=4] {'lat','dep'}, dimensions={0} | all-to-all | bytes 1572864 | tf_op jit(solution)/shard_map/all_to_all | solution.py:246
  62.4 7.0 %rays.1 = (f32[64,64]{1,0:T(8,128)}, bf16[3072,128]{1,0:T(8,128)(2,1)S(1)}) custom-call(s32[1]{0:T(128)S(6)} %copy.10.count_ref, f32[1,512]{1,0:T(1,128)S(1)} %get-tuple-element.7.slot_ref, bf16[3072,128]{1,0:T(8,128)(2,1)S(1)} %bitcast.14, f32[512,256]{1,0:T(8,128)} %coefficient_hbm.1, f32[64,64]{1,0:T(8,128)} %observed_hbm.1, bf16[512,64,128]{2,1,0:T(8,128)(2,1)} %kernel_ref.1), custom_call_target="tpu_custom_call" | custom-call | tf_op jit(solution)/shard_map/rays/pallas_call | solution.py:291
  69.4 31.7 %all_to_all.17 = bf16[256,3,4,128]{3,2,1,0:T(4,128)(2,1)S(1)} all-to-all(bf16[256,3,4,128]{3,2,1,0:T(4,128)(2,1)S(1)} %bitcast.17), channel_id=1, replica_groups=mesh['lat'=64,'dep'=4] {'lat','dep'}, dimensions={0} | all-to-all | bytes 1572864 | tf_op jit(solution)/shard_map/all_to_all | solution.py:246
  101.1 1.7 %add.1 = f32[4,512,128]{2,1,0:T(8,128)} custom-call(s32[256,128]{1,0:T(8,128)S(1)} %bitcast.16, bf16[3072,128]{1,0:T(8,128)(2,1)S(1)} %bitcast.12), custom_call_target="tpu_custom_call" | custom-call | tf_op jit(solution)/shard_map/add/pallas_call | solution.py:312

commit v6 on v5

--- a/solution.py
+++ b/solution.py
@@ -113,8 +113,9 @@
 
     coefficient_copy = pltpu.make_async_copy(coefficient_hbm, coefficient_ref, small_sems.at[0])
     observed_copy = pltpu.make_async_copy(observed_hbm, observed_ref, small_sems.at[1])
+    fetch(0).start()
     coefficient_copy.start()
-    for i in range(chunks):
+    for i in range(1, chunks):
         fetch(i).start()
     observed_copy.start()
     spread_ref[...] = arrived_ref[...].astype(jnp.float32)

time: 103 us -> 103 us (level)
  no operation moved by 1% of the time
where the time goes in v6:
time: 103 us
  blocking collectives  90.9 us (88%)
  Pallas kernels  10.6 us (10%)
  between operations  1.3 us (1%)
    all_to_all x2, blocking collectives, exchange(): back = lax.all_to_all(sent, AXES, split_axis=0, concat_axis=0, tiled=True)  62.7 us
    all_to_all x1, blocking collectives, per_device(): lax.all_to_all(wanted.reshape(devices, 1, 128), AXES, split_axis=0, conca...  28.2 us
    pallas_call x1, Pallas kernels, per_device(): pl.pallas_call(functools.partial(rays_kernel, per_ray=per_ray, params=par...  6.99 us

profile of v6, /device:TPU:1, one launch (start us, length us, event | category | flops | bytes accessed | tf_op | source)
XLA Modules:
  0.0 102.8 jit_solution(5923850251365581412)
XLA Ops:
  1.3 1.3 %plan.1 = (s32[256,128]{1,0:T(8,128)S(1)}, f32[1,512]{1,0:T(1,128)S(1)}, bf16[512,512]{1,0:T(8,128)(2,1)S(1)}) custom-call(s32[1]{0:T(128)S(6)} %copy.10.count_ref, s32[1,512]{1,0:T(1,128)} %bitcast.21, s32[1,512]{1,0:T(1,128)} %bitcast.22, f32[4,512,128]{2,1,0:T(8,128)} %bitcast.19), custom_call_target="tpu_custom_call" | custom-call | tf_op jit(solution)/shard_map/plan/pallas_call | solution.py:261
  2.6 28.2 %all_to_all.15 = s32[256,1,128]{2,1,0:T(1,128)S(1)} all-to-all(s32[256,1,128]{2,1,0:T(1,128)S(1)} %bitcast.18), channel_id=1, replica_groups=mesh['lat'=64,'dep'=4] {'lat','dep'}, dimensions={0} | all-to-all | bytes 262144 | tf_op jit(solution)/shard_map/all_to_all | solution.py:279
  30.8 0.7 fetch.1
  31.4 31.0 %all_to_all.16 = bf16[256,3,4,128]{3,2,1,0:T(4,128)(2,1)S(1)} all-to-all(bf16[256,3,4,128]{3,2,1,0:T(4,128)(2,1)S(1)} %bitcast.13), channel_id=1, replica_groups=mesh['lat'=64,'dep'=4] {'lat','dep'}, dimensions={0} | all-to-all | bytes 1572864 | tf_op jit(solution)/shard_map/all_to_all | solution.py:247
  62.4 7.0 %rays.1 = (f32[64,64]{1,0:T(8,128)}, bf16[3072,128]{1,0:T(8,128)(2,1)S(1)}) custom-call(s32[1]{0:T(128)S(6)} %copy.10.count_ref, f32[1,512]{1,0:T(1,128)S(1)} %get-tuple-element.7.slot_ref, bf16[3072,128]{1,0:T(8,128)(2,1)S(1)} %bitcast.14, f32[512,256]{1,0:T(8,128)} %coefficient_hbm.1, f32[64,64]{1,0:T(8,128)} %observed_hbm.1, bf16[512,64,128]{2,1,0:T(8,128)(2,1)} %kernel_ref.1), custom_call_target="tpu_custom_call" | custom-call | tf_op jit(solution)/shard_map/rays/pallas_call | solution.py:292
  69.4 31.7 %all_to_all.17 = bf16[256,3,4,128]{3,2,1,0:T(4,128)(2,1)S(1)} all-to-all(bf16[256,3,4,128]{3,2,1,0:T(4,128)(2,1)S(1)} %bitcast.17), channel_id=1, replica_groups=mesh['lat'=64,'dep'=4] {'lat','dep'}, dimensions={0} | all-to-all | bytes 1572864 | tf_op jit(solution)/shard_map/all_to_all | solution.py:247
  101.1 1.7 %add.1 = f32[4,512,128]{2,1,0:T(8,128)} custom-call(s32[256,128]{1,0:T(8,128)S(1)} %bitcast.16, bf16[3072,128]{1,0:T(8,128)(2,1)S(1)} %bitcast.12), custom_call_target="tpu_custom_call" | custom-call | tf_op jit(solution)/shard_map/add/pallas_call | solution.py:313
